TPU v7x, 32 devices: a whole 2x2x4 slice. The times are simulated.
32 devices in a mesh: seq: 4 (over y, x), fsdp: 8 (over z, core).
Axes of the slice: x: 2, y: 2, z: 4, core: 2. Of those that a mesh axis runs over, the one named last changes fastest.
Arguments:
- frames: bfloat16 [8, 2048, 1536], P('fsdp', 'seq'), may hold values from -6 to 6
- lengths: int32 [8], P('fsdp'), may hold values from 512 to 2048, as said below
- gain: float32 [1536], replicated, may hold values from 0.5 to 1.5
- w_pointwise: bfloat16 [1536, 3072], P('fsdp'), may hold values from -0.15625 to 0.15625
- w_depthwise: float32 [31, 1536], replicated, may hold values from -1 to 1
- w_output: bfloat16 [1536, 1536], P('fsdp'), may hold values from -0.15625 to 0.15625
- cotangent: bfloat16 [8, 2048, 1536], P('fsdp', 'seq'), may hold values from -6 to 6
Outputs:
- output: bfloat16 [8, 2048, 1536], P('fsdp', 'seq')
- grad_frames: bfloat16 [8, 2048, 1536], P('fsdp', 'seq')
- grad_pointwise: float32 [1536, 3072], P('fsdp')
- grad_output: float32 [1536, 1536], P('fsdp')
- grad_gain: float32 [1536], replicated
- grad_depthwise: float32 [31, 1536], replicated
Inputs may be any that keep to these rules, and one draw needn't show every extreme that they name: `lengths`: the first utterance fills all 2048 slots.
All inputs are finite; a program needn't handle non-finite values.
Results may differ from a plain program's by a relative error of at most 0.014.
Values may be sent and summed in bfloat16 or wider, within the bound.
No kernel may reach another device: no remote copies, remote signals or barrier semaphores. Data moves between devices by JAX's collectives and lax.ppermute only.
A program may use at most 128 MiB of HBM per device.

v0:
```python
import functools

import jax
import jax.numpy as jnp
from jax import lax
from jax.experimental import pallas as pl
from jax.experimental.pallas import tpu as pltpu
from jax.sharding import PartitionSpec as P

EPS = 1e-05
BF = jnp.bfloat16
F32 = jnp.float32
BOTH = ("seq", "fsdp")
N_SEQ, N_Z, N_CORE = 4, 4, 2
FAR, NEAR = 32, 16
VMEM_LIMIT = 60 * 1024 * 1024


def device_pairs(move):
    def flat(s, z, c):
        return (s * N_Z + z) * N_CORE + c
    return [
        (flat(s, z, c), flat(*move(s, z, c)))
        for s in range(N_SEQ) for z in range(N_Z) for c in range(N_CORE)
    ]


ACROSS = {
    "core": device_pairs(lambda s, z, c: (s, z, 1 - c)),
    "x": device_pairs(lambda s, z, c: (s ^ 1, z, c)),
    "y": device_pairs(lambda s, z, c: (s ^ 2, z, c)),
    "d": device_pairs(lambda s, z, c: (s ^ 3, z, c)),
    "z1": device_pairs(lambda s, z, c: (s, (z + 1) % N_Z, c)),
    "z2": device_pairs(lambda s, z, c: (s, (z + 2) % N_Z, c)),
    "z3": device_pairs(lambda s, z, c: (s, (z + 3) % N_Z, c)),
}


def send(block, way):
    return lax.ppermute(block, BOTH, ACROSS[way])


def part(block, index, size, axis):
    return lax.dynamic_slice_in_dim(block, index * size, size, axis)


def hint(bytes_accessed=1024):
    return pl.CostEstimate(flops=0, bytes_accessed=bytes_accessed, transcendentals=0)


def joined_kernel(behind, where_ref, lifted_ref, *refs):
    own, came, mine, other = refs[0:2], refs[2:4], refs[4:6], refs[6:8]
    w_value_ref, w_gate_ref, value_ref, sig_ref, glu_ref = refs[-5:]
    z, c, valid = where_ref[1], where_ref[2], where_ref[3]
    rows = own[0].shape[0]
    outs = w_value_ref, w_gate_ref
    for source, pieces, core in ((own, mine, c), (came, other, 1 - c)):
        at = pl.multiple_of((z * N_CORE + core) * rows, 64)
        for side in range(2):
            outs[side][pl.ds(at, rows), :] = source[side][...]
        for index, k in enumerate(behind):
            at = (lax.rem(z + N_Z - k, N_Z) * N_CORE + core) * rows
            for n in range(2):
                low = pl.ds(pl.multiple_of(at + n * (rows // 2), 32), rows // 2)
                for side in range(2):
                    outs[side][low, :] = pieces[n][index, side]
    frames = value_ref.shape[0]
    value = jnp.dot(lifted_ref[...], w_value_ref[...], preferred_element_type=F32)
    value_ref[...] = value[FAR:FAR + frames]
    sig = jax.nn.sigmoid(jnp.dot(lifted_ref[...], w_gate_ref[...], preferred_element_type=F32))
    sig_ref[...] = sig[FAR:FAR + frames]
    position = lax.broadcasted_iota(jnp.int32, sig.shape, 0) - FAR
    glu_ref[...] = jnp.where(position < valid, value * sig, 0.0).astype(BF)


def joined_call(j, behind, where, lifted, w_own, w_came, mine, other, buffers):
    extended, width = lifted.shape
    frames = extended - 2 * FAR
    block = width // N_SEQ
    rows = w_own.shape[0]
    whole = lambda a: pl.BlockSpec(a.shape, lambda i, at: (0,) * a.ndim)
    column = lambda n: pl.BlockSpec((n, block), lambda i, at: (0, at[0] ^ j))
    second = pl.BlockSpec((rows, block), lambda i, at: (0, N_SEQ + (at[0] ^ j)))
    operands = [lifted, w_own, w_own, w_came, w_came, *mine, *other]
    specs = [whole(lifted), column(rows), second, column(rows), second]
    specs += [whole(a) for a in (*mine, *other)]
    aliases = {}
    if buffers:
        aliases = {1 + len(operands) + n: n for n in range(5)}
        operands += buffers
        specs += [pl.BlockSpec(memory_space=pl.ANY)] * 5
    return pl.pallas_call(
        functools.partial(joined_kernel, behind),
        grid_spec=pltpu.PrefetchScalarGridSpec(
            num_scalar_prefetch=1, grid=(1,), in_specs=specs,
            out_specs=[column(width), column(width), column(frames), column(frames), column(extended)],
        ),
        out_shape=[
            jax.ShapeDtypeStruct((width, width), BF), jax.ShapeDtypeStruct((width, width), BF),
            jax.ShapeDtypeStruct((frames, width), F32), jax.ShapeDtypeStruct((frames, width), F32),
            jax.ShapeDtypeStruct((extended, width), BF),
        ],
        input_output_aliases=aliases,
        compiler_params=pltpu.CompilerParams(vmem_limit_bytes=VMEM_LIMIT),
        cost_estimate=hint(),
        name="joined_%d" % j,
    )(where, *operands)


LANES = 128
SUB = 8


def tap_sum(ext_ref, wide, first, height, flip):
    total = None
    for o in range(len(wide)):
        rows = ext_ref[pl.ds(first + (o + 1), height), :]
        term = rows.reshape(height // SUB, SUB, LANES) * wide[-1 - o if flip else o][None]
        total = term if total is None else total + term
    return total.reshape(height, LANES)


def widened(taps_ref, lanes):
    return [jnp.broadcast_to(taps_ref[k:k + 1, lanes], (SUB, LANES)) for k in range(taps_ref.shape[0])]


def forward_kernel(glu_ref, taps_ref, swished_ref, slope_ref, ext_ref):
    frames, width = swished_ref.shape
    height = 32

    @pl.loop(0, width // LANES)
    def _(b):
        lanes = pl.ds(pl.multiple_of(b * LANES, LANES), LANES)
        wide = widened(taps_ref, lanes)
        ext_ref[...] = glu_ref[:, lanes].astype(F32)
        for first in range(0, frames + 2 * NEAR, height):
            conv = tap_sum(ext_ref, wide, first, height, False)
            sig = jax.nn.sigmoid(conv)
            slope_ref[first:first + height, lanes] = sig * (1.0 + conv * (1.0 - sig))
            low, high = max(first, NEAR), min(first + height, NEAR + frames)
            swished_ref[low - NEAR:high - NEAR, lanes] = (conv * sig)[low - first:high - first].astype(BF)


def forward_call(glu, taps):
    extended, width = glu.shape
    frames = extended - 2 * FAR
    near = frames + 2 * NEAR
    size = width // N_SEQ
    column = lambda rows: pl.BlockSpec((rows, size), lambda i: (0, i))
    return pl.pallas_call(
        forward_kernel,
        grid=(width // size,),
        out_shape=(jax.ShapeDtypeStruct((frames, width), BF), jax.ShapeDtypeStruct((near, width), F32)),
        in_specs=[column(extended), column(taps.shape[0])],
        out_specs=(column(frames), column(near)),
        scratch_shapes=[pltpu.VMEM((extended, LANES), F32)],
        compiler_params=pltpu.CompilerParams(vmem_limit_bytes=VMEM_LIMIT),
        cost_estimate=hint(),
        name="conv_forward",
    )(glu, taps)


def backward_kernel(where_ref, grad_ref, glu_ref, taps_ref, value_ref, sig_ref, *refs):
    mine_ref, send_ref, value_grad_ref, gate_grad_ref, tap_grad_ref, grad_ext_ref, glu_ext_ref, sum_ref = refs[-8:]
    frames, width = value_ref.shape
    taps = taps_ref.shape[0]
    height = 64
    c, valid = where_ref[2], where_ref[3]

    @pl.loop(0, width // LANES)
    def _(b):
        lanes = pl.ds(pl.multiple_of(b * LANES, LANES), LANES)
        wide = widened(taps_ref, lanes)
        grad_ext_ref[...] = grad_ref[:, lanes].astype(F32)
        glu_ext_ref[...] = glu_ref[:, lanes].astype(F32)

        @pl.loop(0, frames // height)
        def _(i):
            first = pl.multiple_of(i * height, height)
            at = pl.ds(first, height)
            glu_grad = tap_sum(grad_ext_ref, wide, first, height, True)
            position = first + lax.broadcasted_iota(jnp.int32, (height, LANES), 0)
            sig = sig_ref[at, lanes]
            scaled = jnp.where(position < valid, glu_grad, 0.0) * sig
            by_gate = (scaled * value_ref[at, lanes] * (1.0 - sig)).astype(BF)
            scaled = scaled.astype(BF)
            value_grad_ref[at, lanes] = scaled
            gate_grad_ref[at, lanes] = by_gate
            mine_ref[at, lanes] = jnp.where(c == 0, scaled, by_gate)
            send_ref[at, lanes] = jnp.where(c == 0, by_gate, scaled)
        sum_ref[...] = jnp.zeros_like(sum_ref)

        @pl.loop(0, frames // height)
        def _(i):
            first = pl.multiple_of(i * height, height)
            grad = grad_ext_ref[pl.ds(pl.multiple_of(first + NEAR, SUB), height), :]
            for k in range(taps):
                term = grad * glu_ext_ref[pl.ds(first + (NEAR + k + 1), height), :]
                sum_ref[k] += jnp.sum(term.reshape(height // SUB, SUB, LANES), axis=0)

        tap_grad_ref[:, lanes] = jnp.sum(sum_ref[...], axis=1)


def backward_call(j, where, grad, glu, taps, value, sig, buffers):
    frames, width = value.shape
    size = width // N_SEQ
    count = taps.shape[0]
    column = lambda rows: pl.BlockSpec((rows, size), lambda i, at: (0, at[0] ^ j))
    alone = pl.BlockSpec((frames, size), lambda i, at: (0, 0))
    operands = [grad, glu, taps, value, sig]
    specs = [column(a.shape[0]) for a in operands]
    aliases = {}
    if buffers:
        aliases = {1 + len(operands) + n: 2 + n for n in range(3)}
        operands += buffers
        specs += [pl.BlockSpec(memory_space=pl.ANY)] * 3
    small = jax.ShapeDtypeStruct((frames, size), BF)
    full = jax.ShapeDtypeStruct((frames, width), BF)
    mine, sent, *buffers = pl.pallas_call(
        backward_kernel,
        grid_spec=pltpu.PrefetchScalarGridSpec(
            num_scalar_prefetch=1, grid=(1,), in_specs=specs,
            out_specs=[alone, alone, column(frames), column(frames), column(count + 1)],
            scratch_shapes=[
                pltpu.VMEM((grad.shape[0], LANES), F32), pltpu.VMEM((glu.shape[0], LANES), F32),
                pltpu.VMEM((count + 1, SUB, LANES), F32),
            ],
        ),
        out_shape=[small, small, full, full, jax.ShapeDtypeStruct((count + 1, width), F32)],
        input_output_aliases=aliases,
        compiler_params=pltpu.CompilerParams(vmem_limit_bytes=VMEM_LIMIT),
        cost_estimate=hint(),
        name="conv_backward_%d" % j,
    )(where, *operands)
    return mine, sent, buffers


def edges(frames, cotangent):
    devices = lax.axis_size("seq")
    forward = [(i, i + 1) for i in range(devices - 1)]
    backward = [(target, source) for source, target in forward]
    last, first = jnp.concatenate([frames[-FAR:], cotangent[-NEAR:]]), jnp.concatenate([frames[:FAR], cotangent[:NEAR]])
    return lax.ppermute(last, "seq", forward), lax.ppermute(first, "seq", backward)


def transposed_dot(left, right):
    return lax.dot_general(left, right, (((0,), (0,)), ((), ())), preferred_element_type=F32)


def final_kernel(block, where_ref, *refs):
    pieces, (pointwise_ref, output_ref) = refs[:-2], refs[-2:]
    s = where_ref[0]
    width = N_SEQ * block
    for j in range(N_SEQ):
        for side in range(2):
            at = pl.multiple_of(side * width + (s ^ j) * block, 128)
            pointwise_ref[:, pl.ds(at, block)] = pieces[j][side].astype(F32)
        rows = pieces[N_SEQ + j].shape[0]
        output_ref[pl.ds(pl.multiple_of((s ^ j) * rows, 16), rows), :] = pieces[N_SEQ + j][...].astype(F32)


def final_call(where, block, pointwise_pieces, output_pieces):
    width = N_SEQ * block
    rows = pointwise_pieces[0].shape[1]
    vmem = pl.BlockSpec(memory_space=pltpu.VMEM)
    operands = (*pointwise_pieces, *output_pieces)
    return pl.pallas_call(
        functools.partial(final_kernel, block),
        out_shape=(
            jax.ShapeDtypeStruct((rows, 2 * width), F32),
            jax.ShapeDtypeStruct((rows, width), F32),
        ),
        in_specs=[pl.BlockSpec(memory_space=pltpu.SMEM)] + [vmem] * len(operands),
        out_specs=(vmem, vmem),
        compiler_params=pltpu.CompilerParams(vmem_limit_bytes=VMEM_LIMIT),
        cost_estimate=hint(),
        name="final",
    )(where, *operands)


def after(values, *first):
    return lax.optimization_barrier((values, first))[0]


def on_slice(frames, lengths, gain, w_pointwise, w_depthwise, w_output, cotangent):
    frame_count, width = frames.shape[1:]
    taps = w_depthwise.shape[0]
    block = width // N_SEQ
    rows = width // (N_Z * N_CORE)
    s = lax.axis_index("seq")
    z, c = lax.axis_index("fsdp") // N_CORE, lax.axis_index("fsdp") % N_CORE
    where = jnp.stack([s, z, c, lengths[0] - s * frame_count]).astype(jnp.int32)

    first = jnp.stack([
        lax.dynamic_slice_in_dim(w_pointwise, s * block, block, 1),
        lax.dynamic_slice_in_dim(w_pointwise, width + s * block, block, 1),
    ])
    behind = (1, 3, 2)
    group = [send(first, "z%d" % k) for k in behind]
    w_came = send(w_pointwise, "core")
    low, high = edges(frames[0], cotangent[0])
    frames_low, cotangent_low = low[:FAR], low[FAR:]
    frames_high, cotangent_high = high[:FAR], high[FAR:]

    def norm(x):
        x = x.astype(F32)
        center = jnp.mean(x, axis=-1, keepdims=True)
        inverse = lax.rsqrt(jnp.mean((x - center) ** 2, axis=-1, keepdims=True) + EPS)
        return (x - center) * inverse, inverse

    normed, inverse = norm(frames[0])
    lifted = (normed * gain).astype(BF)
    lifted_edges = (norm(jnp.concatenate([frames_low, frames_high], axis=0))[0] * gain).astype(BF)
    lifted_ext = jnp.concatenate([lifted_edges[:FAR], lifted, lifted_edges[FAR:]], axis=0)
    position = jnp.arange(-NEAR, frame_count + NEAR, dtype=jnp.int32)
    mask = (position < where[3]).astype(F32)[:, None]
    branch_grad = (cotangent[0].astype(F32) * mask[NEAR:-NEAR]).astype(BF)
    branch_ext = jnp.concatenate([
        (cotangent_low.astype(F32) * mask[:NEAR]).astype(BF), branch_grad,
        (cotangent_high.astype(F32) * mask[-NEAR:]).astype(BF),
    ], axis=0)
    halves = [jnp.stack([p[:, h * (rows // 2):(h + 1) * (rows // 2)] for p in group]) for h in range(2)]
    (group_1, group_2), lifted, lifted_ext, branch_grad, branch_ext, w_came = lax.optimization_barrier(
        (halves, lifted, lifted_ext, branch_grad, branch_ext, w_came)
    )

    def joined(j, mine, other, buffers):
        return joined_call(j, behind, where, lifted_ext, w_pointwise, w_came, mine, other, buffers)

    x_1, y_2, x_2, y_1 = send(group_1, "x"), send(group_2, "y"), send(group_2, "x"), send(group_1, "y")
    full_output = lax.all_gather(after(w_output, group_2), "fsdp", axis=0, tiled=True)
    group_1_other, group_2_other = send(group_1, "core"), send(group_2, "core")
    lifted_other = send(lifted, "core")
    turned = lifted.T, lifted_other.T
    buffers = joined(0, [group_1, group_2], [group_1_other, group_2_other], [])
    x_1, y_2, turned, buffers = lax.optimization_barrier((x_1, y_2, turned, buffers))

    d_1, d_2 = send(x_1, "y"), send(y_2, "x")
    x_1_other, y_2_other, x_2_other, y_1_other = (
        send(x_1, "core"), send(y_2, "core"), send(x_2, "core"), send(y_1, "core")
    )
    buffers = joined(1, [x_1, x_2], [x_1_other, x_2_other], buffers)
    buffers = joined(2, [y_1, y_2], [y_1_other, y_2_other], buffers)
    d_1, d_2, buffers = lax.optimization_barrier((d_1, d_2, buffers))
    buffers = joined(3, [d_1, d_2], [send(d_1, "core"), send(d_2, "core")], buffers)
    w_value, w_gate, value, gate_sig, glu = buffers

    swished, slope = forward_call(glu, w_depthwise)
    contract = (((1,), (1,)), ((), ()))
    swish_grad = lax.dot_general(branch_ext, full_output, contract, preferred_element_type=F32)
    conv_grad = (swish_grad * slope).astype(BF)

    def backward(j, buffers):
        mine, sent, buffers = backward_call(j, where, conv_grad, glu, w_depthwise, value, gate_sig, buffers)
        other = send(sent, "core")

        def term(left):
            return jnp.dot(left[0], mine, preferred_element_type=F32) + jnp.dot(
                left[1], other, preferred_element_type=F32
            )

        return term, buffers

    term_3, buffers = backward(3, [])
    term_1, buffers = backward(1, buffers)
    far = term_3(turned).astype(BF)
    from_d = send(far, "d")
    swished = after(swished, far)
    term_output = transposed_dot(swished, branch_grad).astype(BF)
    owned_output = lax.psum_scatter(term_output, "fsdp", scatter_dimension=0, tiled=True)
    term_2, buffers = backward(2, after(buffers, far, term_output))
    near_x = term_1(turned).astype(BF)
    from_x = send(near_x, "x")
    term_0, buffers = backward(0, after(buffers, near_x))
    near_y = term_2(turned).astype(BF)
    from_y = send(near_y, "y")
    last = term_0(turned)
    grad_value, grad_gate, tap_grad = buffers

    grad_value, grad_gate, swished = after((grad_value, grad_gate, swished), near_y)
    lifted_grad = lax.dot_general(
        grad_value, w_value, contract, preferred_element_type=F32
    ) + lax.dot_general(grad_gate, w_gate, contract, preferred_element_type=F32)
    small = jnp.concatenate([tap_grad[:taps], jnp.sum(lifted_grad * normed, axis=0)[None]], axis=0)
    small = small + send(small, "core")
    branch = jnp.dot(swished, full_output, preferred_element_type=F32)
    output = (frames[0].astype(F32) + branch).astype(BF)
    scaled = lifted_grad * gain
    norm_grad = inverse * (
        scaled
        - jnp.mean(scaled, axis=-1, keepdims=True)
        - normed * jnp.mean(scaled * normed, axis=-1, keepdims=True)
    )
    grad_frames = (cotangent[0].astype(F32) + norm_grad).astype(BF)
    total = (last + from_x.astype(F32) + from_y.astype(F32) + from_d.astype(F32)).astype(BF)
    total, small, grad_frames, output, owned_output = lax.optimization_barrier(
        (total, small, grad_frames, output, owned_output)
    )

    own = part(total, z, 2 * rows, 0)
    over_z = [send(part(total, (z + k) % N_Z, 2 * rows, 0), "z%d" % k) for k in (2, 1, 3)]
    square = (("x", 1), ("y", 2), ("d", 3))
    small_came = [send(small, way) for way, j in square]
    quarter = rows // N_SEQ
    own_output = part(owned_output, s, quarter, 0)
    output_came = [send(part(owned_output, s ^ j, quarter, 0), way) for way, j in square]
    over_z, own, small, small_came, own_output, output_came = lax.optimization_barrier(
        (over_z, own, small, small_came, own_output, output_came)
    )

    own, own_output = own.astype(F32), own_output.astype(F32)
    for piece in over_z:
        own = own + piece.astype(F32)
    for piece in output_came:
        own_output = own_output + piece.astype(F32)
    own, own_output = own.astype(BF), own_output.astype(BF)
    kept, theirs = part(own, c, rows, 0), part(own, 1 - c, rows, 0)
    swapped = send(theirs, "core")
    pair = jnp.stack([jnp.where(c == 0, kept, swapped), jnp.where(c == 0, swapped, kept)])
    small = (small + small_came[0]) + (small_came[1] + small_came[2])
    pair, small = lax.optimization_barrier((pair, small))
    pieces = [pair] + [send(pair, way) for way, j in square]
    small = small + send(small, "z2")
    small = small + send(small, "z1")
    output_pieces = [own_output] + [send(own_output, way) for way, j in square]
    grad_pointwise, grad_output = final_call(where, block, pieces, output_pieces)
    return (output[None], grad_frames[None], grad_pointwise, grad_output, small[taps], small[:taps])


def extended_plain(block, sides, width):
    for axis, dim in sides:
        count = lax.axis_size(axis)
        forward = [(i, i + 1) for i in range(count - 1)]
        backward = [(target, source) for source, target in forward]
        low = lax.ppermute(
            lax.slice_in_dim(block, block.shape[dim] - width, None, axis=dim), axis, forward
        )
        high = lax.ppermute(lax.slice_in_dim(block, 0, width, axis=dim), axis, backward)
        block = jnp.concatenate([low, block, high], axis=dim)
    return block


def rounded_term(left, right):
    term = lax.dot_general(
        left, right, (((0,), (0,)), ((), ())), preferred_element_type=jnp.float32
    )
    term = lax.optimization_barrier(term.astype(jnp.bfloat16))
    return term.astype(jnp.float32)


def on_any_mesh(frames, lengths, gain, w_pointwise, w_depthwise, w_output, cotangent):
    frame_count = frames.shape[1]
    width = frames.shape[2]
    taps = w_depthwise.shape[0]
    half_width = (taps - 1) // 2
    full_pointwise, full_output = (
        lax.all_gather(w_pointwise, "fsdp", axis=0, tiled=True),
        lax.all_gather(w_output, "fsdp", axis=0, tiled=True),
    )
    as_float = frames[0].astype(jnp.float32)
    center = jnp.mean(as_float, axis=-1, keepdims=True)
    spread = jnp.mean((as_float - center) ** 2, axis=-1, keepdims=True)
    inverse = lax.rsqrt(spread + EPS)
    normed = (as_float - center) * inverse
    lifted = (normed * gain).astype(jnp.bfloat16)
    position = lax.axis_index("seq") * frame_count + jnp.arange(frame_count, dtype=jnp.int32)
    mask = (position < lengths[0]).astype(jnp.float32)[:, None]
    joined = jnp.dot(lifted, full_pointwise, preferred_element_type=jnp.float32)
    value = joined[:, :width]
    gate_sig = jax.nn.sigmoid(joined[:, width:])
    glu = (value * gate_sig * mask).astype(jnp.bfloat16)
    glu_ext = extended_plain(glu[None], (("seq", 1),), half_width)[0].astype(jnp.float32)
    conv = jnp.zeros((frame_count, width), jnp.float32)
    for offset in range(taps):
        conv = conv + w_depthwise[offset] * glu_ext[offset : offset + frame_count]
    conv_sig = jax.nn.sigmoid(conv)
    swished = (conv * conv_sig).astype(jnp.bfloat16)
    branch = jnp.dot(swished, full_output, preferred_element_type=jnp.float32)
    output = (as_float + branch).astype(jnp.bfloat16)
    branch_grad = (cotangent[0].astype(jnp.float32) * mask).astype(jnp.bfloat16)
    swish_grad = lax.dot_general(
        branch_grad, full_output, (((1,), (1,)), ((), ())), preferred_element_type=jnp.float32
    )
    conv_grad = (swish_grad * conv_sig * (1.0 + conv * (1.0 - conv_sig))).astype(jnp.bfloat16)
    grad_ext = extended_plain(conv_grad[None], (("seq", 1),), half_width)[0].astype(jnp.float32)
    conv_grad_f = conv_grad.astype(jnp.float32)
    glu_grad = jnp.zeros((frame_count, width), jnp.float32)
    tap_rows = []
    for offset in range(taps):
        back = taps - 1 - offset
        glu_grad = glu_grad + w_depthwise[offset] * grad_ext[back : back + frame_count]
        tap_rows.append(jnp.sum(conv_grad_f * glu_ext[offset : offset + frame_count], axis=0))
    glu_grad = glu_grad * mask
    joined_grad = jnp.concatenate(
        [glu_grad * gate_sig, glu_grad * value * gate_sig * (1.0 - gate_sig)], axis=-1
    ).astype(jnp.bfloat16)
    lifted_grad = lax.dot_general(
        joined_grad, full_pointwise, (((1,), (1,)), ((), ())), preferred_element_type=jnp.float32
    )
    gain_term = jnp.sum(lifted_grad * normed, axis=0)
    grad_gain, grad_depthwise = lax.psum((gain_term, jnp.stack(tap_rows, axis=0)), ("seq", "fsdp"))
    scaled = lifted_grad * gain
    norm_grad = inverse * (
        scaled
        - jnp.mean(scaled, axis=-1, keepdims=True)
        - normed * jnp.mean(scaled * normed, axis=-1, keepdims=True)
    )
    grad_frames = (cotangent[0].astype(jnp.float32) + norm_grad).astype(jnp.bfloat16)
    term_pointwise = rounded_term(lifted, joined_grad)
    term_output = rounded_term(swished, branch_grad)
    owned = (
        lax.psum_scatter(
            term_pointwise.astype(jnp.bfloat16), "fsdp", scatter_dimension=0, tiled=True
        ).astype(jnp.float32),
        lax.psum_scatter(
            term_output.astype(jnp.bfloat16), "fsdp", scatter_dimension=0, tiled=True
        ).astype(jnp.float32),
    )
    grad_pointwise, grad_output = (
        lax.psum(owned[0].astype(jnp.bfloat16), "seq").astype(jnp.float32),
        lax.psum(owned[1].astype(jnp.bfloat16), "seq").astype(jnp.float32),
    )
    return (output[None], grad_frames[None], grad_pointwise, grad_output, grad_gain, grad_depthwise)


def solution(mesh):
    in_specs = (
        P("fsdp", "seq", None),
        P("fsdp"),
        P(),
        P("fsdp", None),
        P(),
        P("fsdp", None),
        P("fsdp", "seq", None),
    )
    out_specs = (
        P("fsdp", "seq", None),
        P("fsdp", "seq", None),
        P("fsdp", None),
        P("fsdp", None),
        P(),
        P(),
    )
    known = mesh.shape["seq"] == N_SEQ and mesh.shape["fsdp"] == N_Z * N_CORE
    return jax.shard_map(
        on_slice if known else on_any_mesh,
        mesh=mesh, in_specs=in_specs, out_specs=out_specs, check_vma=False,
    )
```

profile of v0, /device:TPU:0, one launch (start us, length us, event | category | flops | bytes accessed | tf_op | source)
XLA Modules:
  0.0 267.4 jit_solution(11894631252109692375)
XLA Ops:
  8.4 3.1 %collective-permute-start = (bf16[2,192,384]{2,1,0:T(8,128)(2,1)S(1)}, bf16[2,192,384]{2,1,0:T(8,128)(2,1)}, u32[]{:S(2)}, u32[]{:S(2)}) collective-permute-start(bf16[2,192,384]{2,1,0:T(8,128)(2,1)S(1)} %pad_maximum_fusion.4), channel_id=1, source_target_pairs={{0,2},{1,3},{2,4},{3,5},{4,6},{5,7},{6,0},{7,1},{8,10},{9,11},{10,... | collective-permute-start | bytes 884744 | tf_op jit(solution)/shard_map/ppermute | solution.py:40
  11.5 2.1 collective-permute-start.1
  17.0 4.0 %collective-permute-start.3 = (bf16[48,1536]{1,0:T(8,128)(2,1)}, bf16[48,1536]{1,0:T(8,128)(2,1)}, u32[]{:S(2)}, u32[]{:S(2)}) collective-permute-start(bf16[48,1536]{1,0:T(8,128)(2,1)} %pad_maximum_fusion.8), channel_id=1, source_target_pairs={{0,8},{8,16},{16,24},{1,9},{9,17},{17,25},{2,10},{10,18},{18,26},{... | collective-permute-start | bytes 442376 | tf_op jit(solution)/shard_map/ppermute | solution.py:243
  24.6 2.3 fusion.8
  37.0 2.6 collective-permute-done.2
  43.4 1.5 collective-permute-start.16
  46.8 1.5 collective-permute-start.7
  49.1 7.5 %collective-permute-done.16.refs_5_ = bf16[3,2,96,384]{3,2,1,0:T(8,128)(2,1)} collective-permute-done((bf16[3,2,96,384]{3,2,1,0:T(8,128)(2,1)}, bf16[3,2,96,384]{3,2,1,0:T(8,128)(2,1)}, u32[]{:S(2)}, u32[]{:S(2)}) %collective-permute-start.16) | collective-permute-done | bytes 442400 | tf_op jit(solution)/shard_map/ppermute | solution.py:40
  57.3 6.1 %joined_0.1 = (bf16[1536,1536]{1,0:T(8,128)(2,1)}, bf16[1536,1536]{1,0:T(8,128)(2,1)}, f32[512,1536]{1,0:T(8,128)}, f32[512,1536]{1,0:T(8,128)}, bf16[576,1536]{1,0:T(8,128)(2,1)}) custom-call(s32[4]{0:T(128)} %pad_add_fusion.where_ref, bf16[576,1536]{1,0:T(8,128)(2,1)} %pad_maximum_fusion.lifted_ref, bf16[192,3072]{1,0:T(8,128)(2,1)} %refs_1_.7, ...), custom_call_target="tpu_custom_call" | custom-call | bytes 1024 | tf_op jit(solution)/shard_map/joined_0/pallas_call | solution.py:92
  63.5 2.2 collective-permute-done.6.refs_4_
  65.7 3.3 %collective-permute-done.13.refs_4_ = bf16[3,2,96,384]{3,2,1,0:T(8,128)(2,1)} collective-permute-done((bf16[3,2,96,384]{3,2,1,0:T(8,128)(2,1)}, bf16[3,2,96,384]{3,2,1,0:T(8,128)(2,1)}, u32[]{:S(2)}, u32[]{:S(2)}) %collective-permute-start.13) | collective-permute-done | bytes 442400 | tf_op jit(solution)/shard_map/ppermute | solution.py:40
  69.6 1.5 collective-permute-start.11
  71.1 1.5 collective-permute-start.12
  72.6 6.2 %joined_1.1 = (bf16[1536,1536]{1,0:T(8,128)(2,1)}, bf16[1536,1536]{1,0:T(8,128)(2,1)}, f32[512,1536]{1,0:T(8,128)}, f32[512,1536]{1,0:T(8,128)}, bf16[576,1536]{1,0:T(8,128)(2,1)}) custom-call(s32[4]{0:T(128)} %pad_add_fusion.where_ref, ...), custom_call_target="tpu_custom_call", output_to_operand_aliasing={{0}: (10, {}), {1}: (11, {}), {2}: (12, {}), {3}: (13, {}),... | custom-call | bytes 1024 | tf_op jit(solution)/shard_map/joined_1/pallas_call | solution.py:92
  78.8 6.1 %joined_2.1 = (bf16[1536,1536]{1,0:T(8,128)(2,1)}, bf16[1536,1536]{1,0:T(8,128)(2,1)}, f32[512,1536]{1,0:T(8,128)}, f32[512,1536]{1,0:T(8,128)}, bf16[576,1536]{1,0:T(8,128)(2,1)}) custom-call(s32[4]{0:T(128)} %pad_add_fusion.where_ref, ...), custom_call_target="tpu_custom_call", output_to_operand_aliasing={{0}: (10, {}), {1}: (11, {}), {2}: (12, {}), {3}: (13, {}),... | custom-call | bytes 1024 | tf_op jit(solution)/shard_map/joined_2/pallas_call | solution.py:92
  88.0 6.1 %joined_3.1 = (bf16[1536,1536]{1,0:T(8,128)(2,1)}, bf16[1536,1536]{1,0:T(8,128)(2,1)}, f32[512,1536]{1,0:T(8,128)}, f32[512,1536]{1,0:T(8,128)}, bf16[576,1536]{1,0:T(8,128)(2,1)}) custom-call(s32[4]{0:T(128)} %pad_add_fusion.where_ref, ...), custom_call_target="tpu_custom_call", output_to_operand_aliasing={{0}: (10, {}), {1}: (11, {}), {2}: (12, {}), {3}: (13, {}),... | custom-call | bytes 1024 | tf_op jit(solution)/shard_map/joined_3/pallas_call | solution.py:92
  94.1 10.2 %conv_forward.1 = (bf16[512,1536]{1,0:T(8,128)(2,1)}, f32[544,1536]{1,0:T(8,128)}) custom-call(bf16[576,1536]{1,0:T(8,128)(2,1)} %get-tuple-element.140.glu_ref, f32[31,1536]{1,0:T(8,128)} %taps_ref.9), custom_call_target="tpu_custom_call" | custom-call | bytes 1024 | tf_op jit(solution)/shard_map/conv_forward/pallas_call | solution.py:150
  104.3 7.8 %fusion.18.grad_ref = bf16[544,1536]{1,0:T(8,128)(2,1)} fusion(f32[544,1536]{1,0:T(8,128)} %get-tuple-element.141, bf16[544,1536]{1,0:T(8,128)(2,1)} %pad_maximum_fusion.1, bf16[1536,1536]{1,0:T(8,128)(2,1)} %all-gather.2.cloned.1.call-done), kind=kOutput, calls=%fused_computation.29 | convolution fusion | flops 2568585216 | bytes 11403264 | tf_op jit(solution)/shard_map/dot_general | solution.py:350
  112.1 7.9 %conv_backward_3.1 = (bf16[512,384]{1,0:T(8,128)(2,1)}, bf16[512,384]{1,0:T(8,128)(2,1)}, bf16[512,1536]{1,0:T(8,128)(2,1)}, bf16[512,1536]{1,0:T(8,128)(2,1)}, f32[32,1536]{1,0:T(8,128)}) custom-call(s32[4]{0:T(128)} %pad_add_fusion.where_ref, bf16[544,1536]{1,0:T(8,128)(2,1)} %fusion.18.grad_ref, bf16[576,1536]{1,0:T(8,128)(2,1)} %get-tuple-element.140.glu_ref, ...), custom_call_target="tpu_custom_call" | custom-call | bytes 1024 | tf_op jit(solution)/shard_map/conv_backward_3/pallas_call | solution.py:219
  120.2 1.8 collective-permute-done.21
  123.0 2.1 fusion.21
  125.1 4.4 %convolution_convert_fusion = bf16[1536,1536]{1,0:T(8,128)(2,1)} fusion(bf16[512,1536]{1,0:T(8,128)(2,1)S(1)} %copy-done.28, bf16[512,1536]{1,0:T(8,128)(2,1)S(1)} %copy-done.8), kind=kOutput, calls=%fused_computation | convolution fusion | flops 2418278400 | bytes 7864320 | tf_op jit(solution)/shard_map/dot_general | solution.py:247
  129.5 7.9 %conv_backward_1.1 = (bf16[512,384]{1,0:T(8,128)(2,1)}, bf16[512,384]{1,0:T(8,128)(2,1)}, bf16[512,1536]{1,0:T(8,128)(2,1)}, bf16[512,1536]{1,0:T(8,128)(2,1)}, f32[32,1536]{1,0:T(8,128)}) custom-call(s32[4]{0:T(128)} %pad_add_fusion.where_ref, bf16[544,1536]{1,0:T(8,128)(2,1)} %fusion.18.grad_ref, ...), custom_call_target="tpu_custom_call", output_to_operand_aliasing={{2}: (6, {}), {3}: (7, {}), {4}: (8, {})} | custom-call | bytes 1024 | tf_op jit(solution)/shard_map/conv_backward_1/pallas_call | solution.py:219
  138.0 8.0 %conv_backward_2.1 = (bf16[512,384]{1,0:T(8,128)(2,1)}, bf16[512,384]{1,0:T(8,128)(2,1)}, bf16[512,1536]{1,0:T(8,128)(2,1)}, bf16[512,1536]{1,0:T(8,128)(2,1)}, f32[32,1536]{1,0:T(8,128)}) custom-call(s32[4]{0:T(128)} %pad_add_fusion.where_ref, bf16[544,1536]{1,0:T(8,128)(2,1)} %fusion.18.grad_ref, ...), custom_call_target="tpu_custom_call", output_to_operand_aliasing={{2}: (6, {}), {3}: (7, {}), {4}: (8, {})} | custom-call | bytes 1024 | tf_op jit(solution)/shard_map/conv_backward_2/pallas_call | solution.py:219
  147.0 2.1 fusion.22
  150.3 8.0 %conv_backward_0.1 = (bf16[512,384]{1,0:T(8,128)(2,1)}, bf16[512,384]{1,0:T(8,128)(2,1)}, bf16[512,1536]{1,0:T(8,128)(2,1)}, bf16[512,1536]{1,0:T(8,128)(2,1)}, f32[32,1536]{1,0:T(8,128)}) custom-call(s32[4]{0:T(128)} %pad_add_fusion.where_ref, bf16[544,1536]{1,0:T(8,128)(2,1)} %fusion.18.grad_ref, ...), custom_call_target="tpu_custom_call", output_to_operand_aliasing={{2}: (6, {}), {3}: (7, {}), {4}: (8, {})} | custom-call | bytes 1024 | tf_op jit(solution)/shard_map/conv_backward_0/pallas_call | solution.py:219
  160.6 1.9 collective-permute-start.26
  162.5 4.9 %fusion.37 = f32[512,1536]{1,0:T(8,128)S(1)} fusion(bf16[512,1536]{1,0:T(8,128)(2,1)S(1)} %copy-done.5, bf16[1536,1536]{1,0:T(8,128)(2,1)} %get-tuple-element.177), kind=kOutput, calls=%fused_computation.98 | convolution fusion | flops 2415919104 | bytes 9437184 | tf_op jit(solution)/shard_map/dot_general | solution.py:383
  167.5 3.2 %fusion.10 = (f32[512]{0:T(512)S(1)}, f32[1536]{0:T(1024)S(1)}, f32[512]{0:T(512)S(1)}, f32[512,1536]{1,0:T(8,128)S(1)}) fusion(bf16[1,512,1536]{2,1,0:T(8,128)(2,1)S(1)} %copy-done.3, f32[1536]{0:T(1024)S(1)} %copy-done.27, f32[512]{0:T(512)S(1)} %add_rsqrt_fusion, f32[512]{0:T(512)S(1)} %broadcast_multiply_fusion.2, f32[512,1536]{1,0:T(8,128)S(1)} %fusion.37, ...), kind=kOutput, calls=%fused_computation.17 | convolution fusion | flops 2423780864 | bytes 14176256 | tf_op jit(solution)/shard_map/dot_general | solution.py:381
  170.9 3.7 %fusion.19 = bf16[512,1536]{1,0:T(8,128)(2,1)} fusion(bf16[512,1536]{1,0:T(8,128)(2,1)S(1)} %copy-done.29, bf16[1536,1536]{1,0:T(8,128)(2,1)S(1)} %bitcast.121, bf16[1,512,1536]{2,1,0:T(8,128)(2,1)S(1)} %copy-done.3), kind=kOutput, calls=%fused_computation.30 | convolution fusion | flops 2418278400 | bytes 9437184 | tf_op jit(solution)/shard_map/dot_general | solution.py:386
  174.7 2.5 fusion.15
  178.2 12.8 %collective-permute-done.24 = bf16[1536,384]{1,0:T(8,128)(2,1)} collective-permute-done((bf16[1536,384]{1,0:T(8,128)(2,1)}, bf16[1536,384]{1,0:T(8,128)(2,1)}, u32[]{:S(2)}, u32[]{:S(2)}) %collective-permute-start.24) | collective-permute-done | bytes 1179680 | tf_op jit(solution)/shard_map/ppermute | solution.py:40
  192.2 3.0 %fusion.24 = bf16[1536,384]{1,0:T(8,128)(2,1)S(1)} fusion(f32[1536,384]{1,0:T(8,128)S(1)} %fusion.35, bf16[1536,512]{0,1:T(8,128)(2,1)S(1)} %bitcast.113, bf16[512,384]{1,0:T(8,128)(2,1)S(1)} %copy-done.14, bf16[1536,384]{1,0:T(8,128)(2,1)} %collective-permute-done.27, bf16[1536,384]{1,0:T(8,128)(2,1)S(1)} %collective-permute-done.26, ...), kind=kOutput, calls=%fused_computation.35 | convolution fusion | flops 608698368 | bytes 9043968 | tf_op jit(solution)/shard_map/dot_general | solution.py:358
  195.3 1.9 constant_dynamic-slice_fusion.1
  198.1 2.6 collective-permute-start.37
  201.3 2.9 %collective-permute-done.35 = bf16[48,1536]{1,0:T(8,128)(2,1)} collective-permute-done((bf16[48,1536]{1,0:T(8,128)(2,1)}, bf16[48,1536]{1,0:T(8,128)(2,1)}, u32[]{:S(2)}, u32[]{:S(2)}) %collective-permute-start.35) | collective-permute-done | bytes 147488 | tf_op jit(solution)/shard_map/ppermute | solution.py:40
  205.3 2.7 %collective-permute-start.31 = (bf16[384,384]{1,0:T(8,128)(2,1)S(1)}, bf16[384,384]{1,0:T(8,128)(2,1)S(1)}, u32[]{:S(2)}, u32[]{:S(2)}) collective-permute-start(bf16[384,384]{1,0:T(8,128)(2,1)S(1)} %get-tuple-element.208), channel_id=1, source_target_pairs={{0,6},{1,7},{2,0},{3,1},{4,2},{5,3},{6,4},{7,5},{8,14},{9,15},{10,... | collective-permute-start | bytes 884744 | tf_op jit(solution)/shard_map/ppermute | solution.py:40
  208.8 1.7 collective-permute-done.32
  211.1 6.8 %collective-permute-done.33 = f32[32,1536]{1,0:T(8,128)S(1)} collective-permute-done((f32[32,1536]{1,0:T(8,128)S(1)}, f32[32,1536]{1,0:T(8,128)S(1)}, u32[]{:S(2)}, u32[]{:S(2)}) %collective-permute-start.33) | collective-permute-done | bytes 196640 | tf_op jit(solution)/shard_map/ppermute | solution.py:40
  217.9 3.7 %collective-permute-done.29 = bf16[384,384]{1,0:T(8,128)(2,1)S(1)} collective-permute-done((bf16[384,384]{1,0:T(8,128)(2,1)S(1)}, bf16[384,384]{1,0:T(8,128)(2,1)S(1)}, u32[]{:S(2)}, u32[]{:S(2)}) %collective-permute-start.29) | collective-permute-done | bytes 294944 | tf_op jit(solution)/shard_map/ppermute | solution.py:40
  221.6 2.8 %collective-permute-done.31 = bf16[384,384]{1,0:T(8,128)(2,1)S(1)} collective-permute-done((bf16[384,384]{1,0:T(8,128)(2,1)S(1)}, bf16[384,384]{1,0:T(8,128)(2,1)S(1)}, u32[]{:S(2)}, u32[]{:S(2)}) %collective-permute-start.31) | collective-permute-done | bytes 294944 | tf_op jit(solution)/shard_map/ppermute | solution.py:40
  226.2 4.8 %collective-permute-start.45 = (f32[32,1536]{1,0:T(8,128)S(1)}, f32[32,1536]{1,0:T(8,128)S(1)}, u32[]{:S(2)}, u32[]{:S(2)}) collective-permute-start(f32[32,1536]{1,0:T(8,128)S(1)} %add_add_fusion), channel_id=1, source_target_pairs={{0,4},{1,5},{2,6},{3,7},{4,0},{5,1},{6,2},{7,3},{8,12},{9,13},{10,... | collective-permute-start | bytes 589832 | tf_op jit(solution)/shard_map/ppermute | solution.py:40
  232.1 1.8 collective-permute-start.42
  236.2 4.2 %collective-permute-done.45 = f32[32,1536]{1,0:T(8,128)S(1)} collective-permute-done((f32[32,1536]{1,0:T(8,128)S(1)}, f32[32,1536]{1,0:T(8,128)S(1)}, u32[]{:S(2)}, u32[]{:S(2)}) %collective-permute-start.45) | collective-permute-done | bytes 196640 | tf_op jit(solution)/shard_map/ppermute | solution.py:40
  240.4 1.5 collective-permute-start.41
  242.0 1.5 collective-permute-start.44
  243.6 10.2 %collective-permute-done.44.refs_7_ = bf16[48,1536]{1,0:T(8,128)(2,1)S(1)} collective-permute-done((bf16[48,1536]{1,0:T(8,128)(2,1)S(1)}, bf16[48,1536]{1,0:T(8,128)(2,1)S(1)}, u32[]{:S(2)}, u32[]{:S(2)}) %collective-permute-start.44) | collective-permute-done | bytes 147488 | tf_op jit(solution)/shard_map/ppermute | solution.py:40
  256.5 3.4 %final.1 = (f32[192,3072]{1,0:T(8,128)}, f32[192,1536]{1,0:T(8,128)}) custom-call(s32[4]{0:T(128)} %pad_add_fusion.where_ref, bf16[2,192,384]{2,1,0:T(8,128)(2,1)} %copy-done.10, bf16[2,192,384]{2,1,0:T(8,128)(2,1)} %copy-done.18, bf16[2,192,384]{2,1,0:T(8,128)(2,1)} %copy-done.19, bf16[2,192,384]{2,1,0:T(8,128)(2,1)} %copy-done.20, ...), custom_call_target="tpu_custom_call" | custom-call | bytes 1024 | tf_op jit(solution)/shard_map/final/pallas_call | solution.py:267
  (193 shorter events, 49.6 us)
Async XLA Ops:
  7.2 97.1 %all-gather.2.cloned.1.call-start = ((), (), s32[]{:S(2)}) async-start(), calls=%async_computation.1 | async-start | bytes 5308416 | tf_op jit(solution)/shard_map/all_gather | solution.py:331
  8.4 26.5 %collective-permute-start = (bf16[2,192,384]{2,1,0:T(8,128)(2,1)S(1)}, bf16[2,192,384]{2,1,0:T(8,128)(2,1)}, u32[]{:S(2)}, u32[]{:S(2)}) collective-permute-start(bf16[2,192,384]{2,1,0:T(8,128)(2,1)S(1)} %pad_maximum_fusion.4), channel_id=1, source_target_pairs={{0,2},{1,3},{2,4},{3,5},{4,6},{5,7},{6,0},{7,1},{8,10},{9,11},{10,... | collective-permute-start | bytes 884744 | tf_op jit(solution)/shard_map/ppermute | solution.py:40
  11.5 24.5 %collective-permute-start.1 = (bf16[2,192,384]{2,1,0:T(8,128)(2,1)S(1)}, bf16[2,192,384]{2,1,0:T(8,128)(2,1)}, u32[]{:S(2)}, u32[]{:S(2)}) collective-permute-start(bf16[2,192,384]{2,1,0:T(8,128)(2,1)S(1)} %pad_maximum_fusion.4), channel_id=1, source_target_pairs={{0,6},{1,7},{2,0},{3,1},{4,2},{5,3},{6,4},{7,5},{8,14},{9,15},{10,... | collective-permute-start | bytes 884744 | tf_op jit(solution)/shard_map/ppermute | solution.py:40
  13.6 26.0 %collective-permute-start.2 = (bf16[2,192,384]{2,1,0:T(8,128)(2,1)S(1)}, bf16[2,192,384]{2,1,0:T(8,128)(2,1)}, u32[]{:S(2)}, u32[]{:S(2)}) collective-permute-start(bf16[2,192,384]{2,1,0:T(8,128)(2,1)S(1)} %pad_maximum_fusion.4), channel_id=1, source_target_pairs={{0,4},{1,5},{2,6},{3,7},{4,0},{5,1},{6,2},{7,3},{8,12},{9,13},{10,... | collective-permute-start | bytes 884744 | tf_op jit(solution)/shard_map/ppermute | solution.py:40
  17.0 10.0 %collective-permute-start.3 = (bf16[48,1536]{1,0:T(8,128)(2,1)}, bf16[48,1536]{1,0:T(8,128)(2,1)}, u32[]{:S(2)}, u32[]{:S(2)}) collective-permute-start(bf16[48,1536]{1,0:T(8,128)(2,1)} %pad_maximum_fusion.8), channel_id=1, source_target_pairs={{0,8},{8,16},{16,24},{1,9},{9,17},{17,25},{2,10},{10,18},{18,26},{... | collective-permute-start | bytes 442376 | tf_op jit(solution)/shard_map/ppermute | solution.py:243
  21.7 7.3 %collective-permute-start.4 = (bf16[48,1536]{1,0:T(8,128)(2,1)}, bf16[48,1536]{1,0:T(8,128)(2,1)}, u32[]{:S(2)}, u32[]{:S(2)}) collective-permute-start(bf16[48,1536]{1,0:T(8,128)(2,1)} %pad_maximum_fusion.9), channel_id=1, source_target_pairs={{8,0},{16,8},{24,16},{9,1},{17,9},{25,17},{10,2},{18,10},{26,18},{... | collective-permute-start | bytes 442376 | tf_op jit(solution)/shard_map/ppermute | solution.py:243
  27.0 14.6 %collective-permute-start.5 = (bf16[192,3072]{1,0:T(8,128)(2,1)S(1)}, bf16[192,3072]{1,0:T(8,128)(2,1)S(1)}, u32[]{:S(2)}, u32[]{:S(2)}) collective-permute-start(bf16[192,3072]{1,0:T(8,128)(2,1)S(1)} %copy-done), channel_id=1, source_target_pairs={{0,1},{1,0},{2,3},{3,2},{4,5},{5,4},{6,7},{7,6},{8,9},{9,8},{10,11... | collective-permute-start | bytes 3538952 | tf_op jit(solution)/shard_map/ppermute | solution.py:40
  42.7 152.6 %reduce-scatter.2.cloned.1.call-start = ((), (), s32[]{:S(2)}) async-start(), calls=%async_computation.2 | async-start | bytes 5308416 | tf_op jit(solution)/shard_map/reduce_scatter | solution.py:370
  42.7 23.0 %collective-permute-start.8 = (bf16[512,1536]{1,0:T(8,128)(2,1)S(1)}, bf16[512,1536]{1,0:T(8,128)(2,1)S(1)}, u32[]{:S(2)}, u32[]{:S(2)}) collective-permute-start(bf16[512,1536]{1,0:T(8,128)(2,1)S(1)} %get-tuple-element.105), channel_id=1, source_target_pairs={{0,1},{1,0},{2,3},{3,2},{4,5},{5,4},{6,7},{7,6},{8,9},{9,8},{10,11... | collective-permute-start | bytes 4718600 | tf_op jit(solution)/shard_map/ppermute | solution.py:40
  42.8 4.0 %collective-permute-start.10 = (bf16[3,2,96,384]{3,2,1,0:T(8,128)(2,1)}, bf16[3,2,96,384]{3,2,1,0:T(8,128)(2,1)}, u32[]{:S(2)}, u32[]{:S(2)}) collective-permute-start(bf16[3,2,96,384]{3,2,1,0:T(8,128)(2,1)} %get-tuple-element.104.refs_5_), channel_id=1, source_target_pairs={{0,1},{1,0},{2,3},{3,2},{4,5},{5,4},{6,7},{7,6},{8,9},{9,8},{10,11... | collective-permute-start | bytes 1327112 | tf_op jit(solution)/shard_map/ppermute | solution.py:40
  43.3 5.1 %collective-permute-start.9 = (bf16[3,2,96,384]{3,2,1,0:T(8,128)(2,1)}, bf16[3,2,96,384]{3,2,1,0:T(8,128)(2,1)}, u32[]{:S(2)}, u32[]{:S(2)}) collective-permute-start(bf16[3,2,96,384]{3,2,1,0:T(8,128)(2,1)} %get-tuple-element.103.refs_4_), channel_id=1, source_target_pairs={{0,1},{1,0},{2,3},{3,2},{4,5},{5,4},{6,7},{7,6},{8,9},{9,8},{10,11... | collective-permute-start | bytes 1327112 | tf_op jit(solution)/shard_map/ppermute | solution.py:40
  43.4 13.3 %collective-permute-start.16 = (bf16[3,2,96,384]{3,2,1,0:T(8,128)(2,1)}, bf16[3,2,96,384]{3,2,1,0:T(8,128)(2,1)}, u32[]{:S(2)}, u32[]{:S(2)}) collective-permute-start(bf16[3,2,96,384]{3,2,1,0:T(8,128)(2,1)} %get-tuple-element.104.refs_5_), channel_id=1, source_target_pairs={{0,8},{1,9},{2,10},{3,11},{4,12},{5,13},{6,14},{7,15},{8,0},{9,1},... | collective-permute-start | bytes 1327112 | tf_op jit(solution)/shard_map/ppermute | solution.py:40
  44.9 20.8 %collective-permute-start.6 = (bf16[3,2,96,384]{3,2,1,0:T(8,128)(2,1)}, bf16[3,2,96,384]{3,2,1,0:T(8,128)(2,1)}, u32[]{:S(2)}, u32[]{:S(2)}) collective-permute-start(bf16[3,2,96,384]{3,2,1,0:T(8,128)(2,1)} %get-tuple-element.103.refs_4_), channel_id=1, source_target_pairs={{0,8},{1,9},{2,10},{3,11},{4,12},{5,13},{6,14},{7,15},{8,0},{9,1},... | collective-permute-start | bytes 1327112 | tf_op jit(solution)/shard_map/ppermute | solution.py:40
  46.8 18.9 %collective-permute-start.7 = (bf16[3,2,96,384]{3,2,1,0:T(8,128)(2,1)}, bf16[3,2,96,384]{3,2,1,0:T(8,128)(2,1)}, u32[]{:S(2)}, u32[]{:S(2)}) collective-permute-start(bf16[3,2,96,384]{3,2,1,0:T(8,128)(2,1)} %get-tuple-element.104.refs_5_), channel_id=1, source_target_pairs={{0,16},{1,17},{2,18},{3,19},{4,20},{5,21},{6,22},{7,23},{8,24},{9,... | collective-permute-start | bytes 1327112 | tf_op jit(solution)/shard_map/ppermute | solution.py:40
  48.4 20.7 %collective-permute-start.13 = (bf16[3,2,96,384]{3,2,1,0:T(8,128)(2,1)}, bf16[3,2,96,384]{3,2,1,0:T(8,128)(2,1)}, u32[]{:S(2)}, u32[]{:S(2)}) collective-permute-start(bf16[3,2,96,384]{3,2,1,0:T(8,128)(2,1)} %get-tuple-element.103.refs_4_), channel_id=1, source_target_pairs={{0,16},{1,17},{2,18},{3,19},{4,20},{5,21},{6,22},{7,23},{8,24},{9,... | collective-permute-start | bytes 1327112 | tf_op jit(solution)/shard_map/ppermute | solution.py:40
  56.7 14.4 %collective-permute-start.18 = (bf16[3,2,96,384]{3,2,1,0:T(8,128)(2,1)}, bf16[3,2,96,384]{3,2,1,0:T(8,128)(2,1)}, u32[]{:S(2)}, u32[]{:S(2)}) collective-permute-start(bf16[3,2,96,384]{3,2,1,0:T(8,128)(2,1)} %collective-permute-done.16.refs_5_), channel_id=1, source_target_pairs={{0,1},{1,0},{2,3},{3,2},{4,5},{5,4},{6,7},{7,6},{8,9},{9,8},{10,11... | collective-permute-start | bytes 1327112 | tf_op jit(solution)/shard_map/ppermute | solution.py:40
  65.7 6.9 %collective-permute-start.17 = (bf16[3,2,96,384]{3,2,1,0:T(8,128)(2,1)}, bf16[3,2,96,384]{3,2,1,0:T(8,128)(2,1)}, u32[]{:S(2)}, u32[]{:S(2)}) collective-permute-start(bf16[3,2,96,384]{3,2,1,0:T(8,128)(2,1)} %collective-permute-done.6.refs_4_), channel_id=1, source_target_pairs={{0,1},{1,0},{2,3},{3,2},{4,5},{5,4},{6,7},{7,6},{8,9},{9,8},{10,11... | collective-permute-start | bytes 1327112 | tf_op jit(solution)/shard_map/ppermute | solution.py:40
  69.1 9.7 %collective-permute-start.14 = (bf16[3,2,96,384]{3,2,1,0:T(8,128)(2,1)}, bf16[3,2,96,384]{3,2,1,0:T(8,128)(2,1)}, u32[]{:S(2)}, u32[]{:S(2)}) collective-permute-start(bf16[3,2,96,384]{3,2,1,0:T(8,128)(2,1)} %collective-permute-done.13.refs_4_), channel_id=1, source_target_pairs={{0,1},{1,0},{2,3},{3,2},{4,5},{5,4},{6,7},{7,6},{8,9},{9,8},{10,11... | collective-permute-start | bytes 1327112 | tf_op jit(solution)/shard_map/ppermute | solution.py:40
  69.1 9.7 %collective-permute-start.15 = (bf16[3,2,96,384]{3,2,1,0:T(8,128)(2,1)}, bf16[3,2,96,384]{3,2,1,0:T(8,128)(2,1)}, u32[]{:S(2)}, u32[]{:S(2)}) collective-permute-start(bf16[3,2,96,384]{3,2,1,0:T(8,128)(2,1)} %collective-permute-done.7.refs_5_), channel_id=1, source_target_pairs={{0,1},{1,0},{2,3},{3,2},{4,5},{5,4},{6,7},{7,6},{8,9},{9,8},{10,11... | collective-permute-start | bytes 1327112 | tf_op jit(solution)/shard_map/ppermute | solution.py:40
  69.6 15.4 %collective-permute-start.11 = (bf16[3,2,96,384]{3,2,1,0:T(8,128)(2,1)}, bf16[3,2,96,384]{3,2,1,0:T(8,128)(2,1)S(1)}, u32[]{:S(2)}, u32[]{:S(2)}) collective-permute-start(bf16[3,2,96,384]{3,2,1,0:T(8,128)(2,1)} %collective-permute-done.6.refs_4_), channel_id=1, source_target_pairs={{0,16},{1,17},{2,18},{3,19},{4,20},{5,21},{6,22},{7,23},{8,24},{9,... | collective-permute-start | bytes 1327112 | tf_op jit(solution)/shard_map/ppermute | solution.py:40
  71.1 13.8 %collective-permute-start.12 = (bf16[3,2,96,384]{3,2,1,0:T(8,128)(2,1)}, bf16[3,2,96,384]{3,2,1,0:T(8,128)(2,1)}, u32[]{:S(2)}, u32[]{:S(2)}) collective-permute-start(bf16[3,2,96,384]{3,2,1,0:T(8,128)(2,1)} %collective-permute-done.7.refs_5_), channel_id=1, source_target_pairs={{0,8},{1,9},{2,10},{3,11},{4,12},{5,13},{6,14},{7,15},{8,0},{9,1},... | collective-permute-start | bytes 1327112 | tf_op jit(solution)/shard_map/ppermute | solution.py:40
  85.0 1.9 collective-permute-start.19
  85.0 3.0 %collective-permute-start.20 = (bf16[3,2,96,384]{3,2,1,0:T(8,128)(2,1)}, bf16[3,2,96,384]{3,2,1,0:T(8,128)(2,1)}, u32[]{:S(2)}, u32[]{:S(2)}) collective-permute-start(bf16[3,2,96,384]{3,2,1,0:T(8,128)(2,1)} %collective-permute-done.12.refs_5_), channel_id=1, source_target_pairs={{0,1},{1,0},{2,3},{3,2},{4,5},{5,4},{6,7},{7,6},{8,9},{9,8},{10,11... | collective-permute-start | bytes 1327112 | tf_op jit(solution)/shard_map/ppermute | solution.py:40
  120.1 1.9 collective-permute-start.21
  137.5 8.5 %collective-permute-start.22 = (bf16[512,384]{1,0:T(8,128)(2,1)}, bf16[512,384]{1,0:T(8,128)(2,1)S(1)}, u32[]{:S(2)}, u32[]{:S(2)}) collective-permute-start(bf16[512,384]{1,0:T(8,128)(2,1)} %get-tuple-element.163), channel_id=1, source_target_pairs={{0,1},{1,0},{2,3},{3,2},{4,5},{5,4},{6,7},{7,6},{8,9},{9,8},{10,11... | collective-permute-start | bytes 1179656 | tf_op jit(solution)/shard_map/ppermute | solution.py:40
  137.6 53.4 %collective-permute-start.27 = (bf16[1536,384]{1,0:T(8,128)(2,1)}, bf16[1536,384]{1,0:T(8,128)(2,1)}, u32[]{:S(2)}, u32[]{:S(2)}) collective-permute-start(bf16[1536,384]{1,0:T(8,128)(2,1)} %fusion.21), channel_id=1, source_target_pairs={{0,24},{1,25},{2,26},{3,27},{4,28},{5,29},{6,30},{7,31},{8,16},{9,... | collective-permute-start | bytes 3538952 | tf_op jit(solution)/shard_map/ppermute | solution.py:40
  145.9 12.6 %collective-permute-start.25 = (bf16[512,384]{1,0:T(8,128)(2,1)}, bf16[512,384]{1,0:T(8,128)(2,1)S(1)}, u32[]{:S(2)}, u32[]{:S(2)}) collective-permute-start(bf16[512,384]{1,0:T(8,128)(2,1)} %get-tuple-element.170), channel_id=1, source_target_pairs={{0,1},{1,0},{2,3},{3,2},{4,5},{5,4},{6,7},{7,6},{8,9},{9,8},{10,11... | collective-permute-start | bytes 1179656 | tf_op jit(solution)/shard_map/ppermute | solution.py:40
  149.1 41.9 %collective-permute-start.24 = (bf16[1536,384]{1,0:T(8,128)(2,1)}, bf16[1536,384]{1,0:T(8,128)(2,1)}, u32[]{:S(2)}, u32[]{:S(2)}) collective-permute-start(bf16[1536,384]{1,0:T(8,128)(2,1)} %fusion.22), channel_id=1, source_target_pairs={{0,8},{1,9},{2,10},{3,11},{4,12},{5,13},{6,14},{7,15},{8,0},{9,1},... | collective-permute-start | bytes 3538952 | tf_op jit(solution)/shard_map/ppermute | solution.py:40
  158.3 18.8 %collective-permute-start.23 = (bf16[512,384]{1,0:T(8,128)(2,1)}, bf16[512,384]{1,0:T(8,128)(2,1)S(1)}, u32[]{:S(2)}, u32[]{:S(2)}) collective-permute-start(bf16[512,384]{1,0:T(8,128)(2,1)} %get-tuple-element.168), channel_id=1, source_target_pairs={{0,1},{1,0},{2,3},{3,2},{4,5},{5,4},{6,7},{7,6},{8,9},{9,8},{10,11... | collective-permute-start | bytes 1179656 | tf_op jit(solution)/shard_map/ppermute | solution.py:40
  160.6 31.6 %collective-permute-start.26 = (bf16[1536,384]{1,0:T(8,128)(2,1)S(1)}, bf16[1536,384]{1,0:T(8,128)(2,1)S(1)}, u32[]{:S(2)}, u32[]{:S(2)}) collective-permute-start(bf16[1536,384]{1,0:T(8,128)(2,1)S(1)} %fusion.23), channel_id=1, source_target_pairs={{0,16},{1,17},{2,18},{3,19},{4,20},{5,21},{6,22},{7,23},{8,24},{9,... | collective-permute-start | bytes 3538952 | tf_op jit(solution)/shard_map/ppermute | solution.py:40
  170.8 7.4 %collective-permute-start.28 = (f32[32,1536]{1,0:T(8,128)S(1)}, f32[32,1536]{1,0:T(8,128)S(1)}, u32[]{:S(2)}, u32[]{:S(2)}) collective-permute-start(f32[32,1536]{1,0:T(8,128)S(1)} %pad_maximum_fusion.7), channel_id=1, source_target_pairs={{0,1},{1,0},{2,3},{3,2},{4,5},{5,4},{6,7},{7,6},{8,9},{9,8},{10,11... | collective-permute-start | bytes 589832 | tf_op jit(solution)/shard_map/ppermute | solution.py:40
  197.2 7.0 %collective-permute-start.35 = (bf16[48,1536]{1,0:T(8,128)(2,1)}, bf16[48,1536]{1,0:T(8,128)(2,1)}, u32[]{:S(2)}, u32[]{:S(2)}) collective-permute-start(bf16[48,1536]{1,0:T(8,128)(2,1)} %get-tuple-element.215), channel_id=1, source_target_pairs={{0,8},{1,9},{2,10},{3,11},{4,12},{5,13},{6,14},{7,15},{8,0},{9,1},... | collective-permute-start | bytes 442376 | tf_op jit(solution)/shard_map/ppermute | solution.py:40
  197.4 8.0 %collective-permute-start.36 = (bf16[48,1536]{1,0:T(8,128)(2,1)}, bf16[48,1536]{1,0:T(8,128)(2,1)}, u32[]{:S(2)}, u32[]{:S(2)}) collective-permute-start(bf16[48,1536]{1,0:T(8,128)(2,1)} %get-tuple-element.214), channel_id=1, source_target_pairs={{0,16},{1,17},{2,18},{3,19},{4,20},{5,21},{6,22},{7,23},{8,24},{9,... | collective-permute-start | bytes 442376 | tf_op jit(solution)/shard_map/ppermute | solution.py:40
  198.1 9.9 %collective-permute-start.37 = (bf16[48,1536]{1,0:T(8,128)(2,1)S(1)}, bf16[48,1536]{1,0:T(8,128)(2,1)S(1)}, u32[]{:S(2)}, u32[]{:S(2)}) collective-permute-start(bf16[48,1536]{1,0:T(8,128)(2,1)S(1)} %get-tuple-element.213), channel_id=1, source_target_pairs={{0,24},{1,25},{2,26},{3,27},{4,28},{5,29},{6,30},{7,31},{8,16},{9,... | collective-permute-start | bytes 442376 | tf_op jit(solution)/shard_map/ppermute | solution.py:40
  200.6 9.9 %collective-permute-start.32 = (f32[32,1536]{1,0:T(8,128)S(1)}, f32[32,1536]{1,0:T(8,128)S(1)}, u32[]{:S(2)}, u32[]{:S(2)}) collective-permute-start(f32[32,1536]{1,0:T(8,128)S(1)} %fusion.64), channel_id=1, source_target_pairs={{0,8},{1,9},{2,10},{3,11},{4,12},{5,13},{6,14},{7,15},{8,0},{9,1},... | collective-permute-start | bytes 589832 | tf_op jit(solution)/shard_map/ppermute | solution.py:40
  201.0 20.7 %collective-permute-start.29 = (bf16[384,384]{1,0:T(8,128)(2,1)S(1)}, bf16[384,384]{1,0:T(8,128)(2,1)S(1)}, u32[]{:S(2)}, u32[]{:S(2)}) collective-permute-start(bf16[384,384]{1,0:T(8,128)(2,1)S(1)} %get-tuple-element.210), channel_id=1, source_target_pairs={{0,4},{1,5},{2,6},{3,7},{4,0},{5,1},{6,2},{7,3},{8,12},{9,13},{10,... | collective-permute-start | bytes 884744 | tf_op jit(solution)/shard_map/ppermute | solution.py:40
  204.2 17.5 %collective-permute-start.30 = (bf16[384,384]{1,0:T(8,128)(2,1)S(1)}, bf16[384,384]{1,0:T(8,128)(2,1)S(1)}, u32[]{:S(2)}, u32[]{:S(2)}) collective-permute-start(bf16[384,384]{1,0:T(8,128)(2,1)S(1)} %get-tuple-element.209), channel_id=1, source_target_pairs={{0,2},{1,3},{2,4},{3,5},{4,6},{5,7},{6,0},{7,1},{8,10},{9,11},{10,... | collective-permute-start | bytes 884744 | tf_op jit(solution)/shard_map/ppermute | solution.py:40
  205.3 19.1 %collective-permute-start.31 = (bf16[384,384]{1,0:T(8,128)(2,1)S(1)}, bf16[384,384]{1,0:T(8,128)(2,1)S(1)}, u32[]{:S(2)}, u32[]{:S(2)}) collective-permute-start(bf16[384,384]{1,0:T(8,128)(2,1)S(1)} %get-tuple-element.208), channel_id=1, source_target_pairs={{0,6},{1,7},{2,0},{3,1},{4,2},{5,3},{6,4},{7,5},{8,14},{9,15},{10,... | collective-permute-start | bytes 884744 | tf_op jit(solution)/shard_map/ppermute | solution.py:40
  208.0 9.9 %collective-permute-start.33 = (f32[32,1536]{1,0:T(8,128)S(1)}, f32[32,1536]{1,0:T(8,128)S(1)}, u32[]{:S(2)}, u32[]{:S(2)}) collective-permute-start(f32[32,1536]{1,0:T(8,128)S(1)} %fusion.64), channel_id=1, source_target_pairs={{0,16},{1,17},{2,18},{3,19},{4,20},{5,21},{6,22},{7,23},{8,24},{9,... | collective-permute-start | bytes 589832 | tf_op jit(solution)/shard_map/ppermute | solution.py:40
  210.6 7.3 %collective-permute-start.34 = (f32[32,1536]{1,0:T(8,128)S(1)}, f32[32,1536]{1,0:T(8,128)S(1)}, u32[]{:S(2)}, u32[]{:S(2)}) collective-permute-start(f32[32,1536]{1,0:T(8,128)S(1)} %fusion.64), channel_id=1, source_target_pairs={{0,24},{1,25},{2,26},{3,27},{4,28},{5,29},{6,30},{7,31},{8,16},{9,... | collective-permute-start | bytes 589832 | tf_op jit(solution)/shard_map/ppermute | solution.py:40
  226.2 14.2 %collective-permute-start.45 = (f32[32,1536]{1,0:T(8,128)S(1)}, f32[32,1536]{1,0:T(8,128)S(1)}, u32[]{:S(2)}, u32[]{:S(2)}) collective-permute-start(f32[32,1536]{1,0:T(8,128)S(1)} %add_add_fusion), channel_id=1, source_target_pairs={{0,4},{1,5},{2,6},{3,7},{4,0},{5,1},{6,2},{7,3},{8,12},{9,13},{10,... | collective-permute-start | bytes 589832 | tf_op jit(solution)/shard_map/ppermute | solution.py:40
  232.1 9.9 %collective-permute-start.42 = (bf16[48,1536]{1,0:T(8,128)(2,1)S(1)}, bf16[48,1536]{1,0:T(8,128)(2,1)S(1)}, u32[]{:S(2)}, u32[]{:S(2)}) collective-permute-start(bf16[48,1536]{1,0:T(8,128)(2,1)S(1)} %add_convert_fusion.1.refs_4_), channel_id=1, source_target_pairs={{0,8},{1,9},{2,10},{3,11},{4,12},{5,13},{6,14},{7,15},{8,0},{9,1},... | collective-permute-start | bytes 442376 | tf_op jit(solution)/shard_map/ppermute | solution.py:40
  233.9 8.1 %collective-permute-start.43 = (bf16[48,1536]{1,0:T(8,128)(2,1)S(1)}, bf16[48,1536]{1,0:T(8,128)(2,1)S(1)}, u32[]{:S(2)}, u32[]{:S(2)}) collective-permute-start(bf16[48,1536]{1,0:T(8,128)(2,1)S(1)} %add_convert_fusion.1.refs_4_), channel_id=1, source_target_pairs={{0,16},{1,17},{2,18},{3,19},{4,20},{5,21},{6,22},{7,23},{8,24},{9,... | collective-permute-start | bytes 442376 | tf_op jit(solution)/shard_map/ppermute | solution.py:40
  234.2 19.6 %collective-permute-start.39 = (bf16[2,192,384]{2,1,0:T(8,128)(2,1)S(1)}, bf16[2,192,384]{2,1,0:T(8,128)(2,1)S(1)}, u32[]{:S(2)}, u32[]{:S(2)}) collective-permute-start(bf16[2,192,384]{2,1,0:T(8,128)(2,1)S(1)} %pad_maximum_fusion.5.refs_0_), channel_id=1, source_target_pairs={{0,8},{1,9},{2,10},{3,11},{4,12},{5,13},{6,14},{7,15},{8,0},{9,1},... | collective-permute-start | bytes 884744 | tf_op jit(solution)/shard_map/ppermute | solution.py:40
  234.8 20.2 %collective-permute-start.40 = (bf16[2,192,384]{2,1,0:T(8,128)(2,1)S(1)}, bf16[2,192,384]{2,1,0:T(8,128)(2,1)S(1)}, u32[]{:S(2)}, u32[]{:S(2)}) collective-permute-start(bf16[2,192,384]{2,1,0:T(8,128)(2,1)S(1)} %pad_maximum_fusion.5.refs_0_), channel_id=1, source_target_pairs={{0,16},{1,17},{2,18},{3,19},{4,20},{5,21},{6,22},{7,23},{8,24},{9,... | collective-permute-start | bytes 884744 | tf_op jit(solution)/shard_map/ppermute | solution.py:40
  240.4 14.6 %collective-permute-start.41 = (bf16[2,192,384]{2,1,0:T(8,128)(2,1)S(1)}, bf16[2,192,384]{2,1,0:T(8,128)(2,1)S(1)}, u32[]{:S(2)}, u32[]{:S(2)}) collective-permute-start(bf16[2,192,384]{2,1,0:T(8,128)(2,1)S(1)} %pad_maximum_fusion.5.refs_0_), channel_id=1, source_target_pairs={{0,24},{1,25},{2,26},{3,27},{4,28},{5,29},{6,30},{7,31},{8,16},{9,... | collective-permute-start | bytes 884744 | tf_op jit(solution)/shard_map/ppermute | solution.py:40
  241.9 18.0 %collective-permute-start.46 = (f32[32,1536]{1,0:T(8,128)S(1)}, f32[32,1536]{1,0:T(8,128)S(1)}, u32[]{:S(2)}, u32[]{:S(2)}) collective-permute-start(f32[32,1536]{1,0:T(8,128)S(1)} %add.206), channel_id=1, source_target_pairs={{0,2},{1,3},{2,4},{3,5},{4,6},{5,7},{6,0},{7,1},{8,10},{9,11},{10,... | collective-permute-start | bytes 589832 | tf_op jit(solution)/shard_map/ppermute | solution.py:40
  242.0 11.8 %collective-permute-start.44 = (bf16[48,1536]{1,0:T(8,128)(2,1)S(1)}, bf16[48,1536]{1,0:T(8,128)(2,1)S(1)}, u32[]{:S(2)}, u32[]{:S(2)}) collective-permute-start(bf16[48,1536]{1,0:T(8,128)(2,1)S(1)} %add_convert_fusion.1.refs_4_), channel_id=1, source_target_pairs={{0,24},{1,25},{2,26},{3,27},{4,28},{5,29},{6,30},{7,31},{8,16},{9,... | collective-permute-start | bytes 442376 | tf_op jit(solution)/shard_map/ppermute | solution.py:40
  (35 other events, 226.0 us)
Sparse Core Ops, SparseCore 0:
  42.8 50.9 all-gather.1
  129.7 52.2 reduce-scatter.1
where the time goes:
time: 268 us; the launch traced here: 267 us
  waiting for transfers between devices  71.9 us (27%)
  Pallas kernels  70 us (26%)
  starting transfers between devices  44.8 us (17%)
  matrix products  36.3 us (14%)
  between operations  15.3 us (6%)
  other arithmetic  15.1 us (6%)
  local copies, waits for them, and re-layouts  14 us (5%)
    ppermute x45, waiting for transfers between devices, send(): return lax.ppermute(block, BOTH, ACROSS[way])  70.8 us
    ppermute x45, starting transfers between devices, send(): return lax.ppermute(block, BOTH, ACROSS[way])  39.4 us
    pallas_call x4, Pallas kernels, backward_call(): pl.pallas_call(backward_kernel, grid_spec=pltpu.PrefetchScalarGridSpec(nu...  31.8 us
    pallas_call x4, Pallas kernels, joined_call(): pl.pallas_call(functools.partial(joined_kernel, behind), grid_spec=pltpu....  24.6 us
    pallas_call x1, Pallas kernels, forward_call(): pl.pallas_call(forward_kernel, grid=(width // size,), out_shape=(jax.Shap...  10.2 us
    dot_general x4, matrix products, term(): jnp.dot(left[0], mine, preferred_element_type=F32)  8.18 us
    dot_general x1, matrix products, on_slice(): lax.dot_general(branch_ext, full_output, contract, preferred_element_type...  7.83 us
  transfers between devices with their start and end apart: 49, of which 21 were waited for; matrix products, arithmetic and copies ran while one was open for 16% of the time, Pallas kernels for 23%

commit v1 on v0

--- a/solution.py
+++ b/solution.py
@@ -333,7 +333,8 @@
     lifted_other = send(lifted, "core")
     turned = lifted.T, lifted_other.T
     buffers = joined(0, [group_1, group_2], [group_1_other, group_2_other], [])
-    x_1, y_2, turned, buffers = lax.optimization_barrier((x_1, y_2, turned, buffers))
+    turned, buffers = lax.optimization_barrier((turned, buffers))
+    x_1, y_2, x_2, y_1, buffers = lax.optimization_barrier((x_1, y_2, x_2, y_1, buffers))
 
     d_1, d_2 = send(x_1, "y"), send(y_2, "x")
     x_1_other, y_2_other, x_2_other, y_1_other = (

time: 268 us -> 266 us (level)
  waiting for transfers between devices: 71.9 us -> 65.3 us
  starting transfers between devices: 44.8 us -> 49.3 us
    ppermute x45, waiting for transfers between devices: 70.8 us -> 64.2 us  [send(): return lax.ppermute(block, BOTH, ACROSS[way])]
    ppermute x45, starting transfers between devices: 39.4 us -> 43.9 us  [send(): return lax.ppermute(block, BOTH, ACROSS[way])]
  transfers between devices with their start and end apart: 49 -> 49, of which waited for: 21 -> 22; matrix products, arithmetic and copies ran while one was open for 16% -> 16% of each run, Pallas kernels for 23% -> 23%
where the time goes in v1:
time: 266 us; the launch traced here: 265 us
  Pallas kernels  69.9 us (26%)
  waiting for transfers between devices  65.3 us (25%)
  starting transfers between devices  49.3 us (19%)
  matrix products  36.3 us (14%)
  between operations  15.3 us (6%)
  other arithmetic  15.1 us (6%)
  local copies, waits for them, and re-layouts  14 us (5%)
    ppermute x45, waiting for transfers between devices, send(): return lax.ppermute(block, BOTH, ACROSS[way])  64.2 us
    ppermute x45, starting transfers between devices, send(): return lax.ppermute(block, BOTH, ACROSS[way])  43.9 us
    pallas_call x4, Pallas kernels, backward_call(): pl.pallas_call(backward_kernel, grid_spec=pltpu.PrefetchScalarGridSpec(nu...  31.8 us
    pallas_call x4, Pallas kernels, joined_call(): pl.pallas_call(functools.partial(joined_kernel, behind), grid_spec=pltpu....  24.5 us
    pallas_call x1, Pallas kernels, forward_call(): pl.pallas_call(forward_kernel, grid=(width // size,), out_shape=(jax.Shap...  10.2 us
    dot_general x4, matrix products, term(): jnp.dot(left[0], mine, preferred_element_type=F32)  8.19 us
    dot_general x1, matrix products, on_slice(): lax.dot_general(branch_ext, full_output, contract, preferred_element_type...  7.82 us
  transfers between devices with their start and end apart: 49, of which 22 were waited for; matrix products, arithmetic and copies ran while one was open for 16% of the time, Pallas kernels for 23%

profile of v1, /device:TPU:0, one launch (start us, length us, event | category | flops | bytes accessed | tf_op | source)
XLA Modules:
  0.0 265.3 jit_solution(12098549048635457610)
XLA Ops:
  8.4 3.1 %collective-permute-start = (bf16[2,192,384]{2,1,0:T(8,128)(2,1)S(1)}, bf16[2,192,384]{2,1,0:T(8,128)(2,1)}, u32[]{:S(2)}, u32[]{:S(2)}) collective-permute-start(bf16[2,192,384]{2,1,0:T(8,128)(2,1)S(1)} %pad_maximum_fusion.4), channel_id=1, source_target_pairs={{0,2},{1,3},{2,4},{3,5},{4,6},{5,7},{6,0},{7,1},{8,10},{9,11},{10,... | collective-permute-start | bytes 884744 | tf_op jit(solution)/shard_map/ppermute | solution.py:40
  11.5 2.1 collective-permute-start.1
  17.0 4.0 %collective-permute-start.3 = (bf16[48,1536]{1,0:T(8,128)(2,1)}, bf16[48,1536]{1,0:T(8,128)(2,1)}, u32[]{:S(2)}, u32[]{:S(2)}) collective-permute-start(bf16[48,1536]{1,0:T(8,128)(2,1)} %pad_maximum_fusion.8), channel_id=1, source_target_pairs={{0,8},{8,16},{16,24},{1,9},{9,17},{17,25},{2,10},{10,18},{18,26},{... | collective-permute-start | bytes 442376 | tf_op jit(solution)/shard_map/ppermute | solution.py:243
  24.6 2.3 fusion.8
  32.2 1.3 pad_maximum_fusion.lifted_ref
  33.6 1.4 pad_maximum_fusion.1
  37.0 2.6 collective-permute-done.2
  43.4 1.5 collective-permute-start.10
  44.9 1.5 collective-permute-start.11
  46.8 1.5 collective-permute-start.12
  48.4 1.5 collective-permute-start.9
  50.5 6.1 %joined_0.1 = (bf16[1536,1536]{1,0:T(8,128)(2,1)}, bf16[1536,1536]{1,0:T(8,128)(2,1)}, f32[512,1536]{1,0:T(8,128)}, f32[512,1536]{1,0:T(8,128)}, bf16[576,1536]{1,0:T(8,128)(2,1)}) custom-call(s32[4]{0:T(128)} %pad_add_fusion.where_ref, bf16[576,1536]{1,0:T(8,128)(2,1)} %pad_maximum_fusion.lifted_ref, bf16[192,3072]{1,0:T(8,128)(2,1)} %refs_1_.7, ...), custom_call_target="tpu_custom_call" | custom-call | bytes 1024 | tf_op jit(solution)/shard_map/joined_0/pallas_call | solution.py:92
  56.7 1.6 collective-permute-done.11.refs_5_
  58.2 7.5 %collective-permute-done.12.refs_4_ = bf16[3,2,96,384]{3,2,1,0:T(8,128)(2,1)} collective-permute-done((bf16[3,2,96,384]{3,2,1,0:T(8,128)(2,1)}, bf16[3,2,96,384]{3,2,1,0:T(8,128)(2,1)}, u32[]{:S(2)}, u32[]{:S(2)}) %collective-permute-start.12) | collective-permute-done | bytes 442400 | tf_op jit(solution)/shard_map/ppermute | solution.py:40
  69.1 1.5 collective-permute-start.14
  70.6 6.2 %joined_1.1 = (bf16[1536,1536]{1,0:T(8,128)(2,1)}, bf16[1536,1536]{1,0:T(8,128)(2,1)}, f32[512,1536]{1,0:T(8,128)}, f32[512,1536]{1,0:T(8,128)}, bf16[576,1536]{1,0:T(8,128)(2,1)}) custom-call(s32[4]{0:T(128)} %pad_add_fusion.where_ref, ...), custom_call_target="tpu_custom_call", output_to_operand_aliasing={{0}: (10, {}), {1}: (11, {}), {2}: (12, {}), {3}: (13, {}),... | custom-call | bytes 1024 | tf_op jit(solution)/shard_map/joined_1/pallas_call | solution.py:92
  76.7 6.1 %joined_2.1 = (bf16[1536,1536]{1,0:T(8,128)(2,1)}, bf16[1536,1536]{1,0:T(8,128)(2,1)}, f32[512,1536]{1,0:T(8,128)}, f32[512,1536]{1,0:T(8,128)}, bf16[576,1536]{1,0:T(8,128)(2,1)}) custom-call(s32[4]{0:T(128)} %pad_add_fusion.where_ref, ...), custom_call_target="tpu_custom_call", output_to_operand_aliasing={{0}: (10, {}), {1}: (11, {}), {2}: (12, {}), {3}: (13, {}),... | custom-call | bytes 1024 | tf_op jit(solution)/shard_map/joined_2/pallas_call | solution.py:92
  85.7 6.1 %joined_3.1 = (bf16[1536,1536]{1,0:T(8,128)(2,1)}, bf16[1536,1536]{1,0:T(8,128)(2,1)}, f32[512,1536]{1,0:T(8,128)}, f32[512,1536]{1,0:T(8,128)}, bf16[576,1536]{1,0:T(8,128)(2,1)}) custom-call(s32[4]{0:T(128)} %pad_add_fusion.where_ref, ...), custom_call_target="tpu_custom_call", output_to_operand_aliasing={{0}: (10, {}), {1}: (11, {}), {2}: (12, {}), {3}: (13, {}),... | custom-call | bytes 1024 | tf_op jit(solution)/shard_map/joined_3/pallas_call | solution.py:92
  91.8 10.2 %conv_forward.1 = (bf16[512,1536]{1,0:T(8,128)(2,1)}, f32[544,1536]{1,0:T(8,128)}) custom-call(bf16[576,1536]{1,0:T(8,128)(2,1)} %get-tuple-element.154.glu_ref, f32[31,1536]{1,0:T(8,128)} %taps_ref.9), custom_call_target="tpu_custom_call" | custom-call | bytes 1024 | tf_op jit(solution)/shard_map/conv_forward/pallas_call | solution.py:150
  102.0 7.8 %fusion.18.grad_ref = bf16[544,1536]{1,0:T(8,128)(2,1)} fusion(f32[544,1536]{1,0:T(8,128)} %get-tuple-element.155, bf16[544,1536]{1,0:T(8,128)(2,1)} %pad_maximum_fusion.1, bf16[1536,1536]{1,0:T(8,128)(2,1)} %all-gather.2.cloned.1.call-done), kind=kOutput, calls=%fused_computation.29 | convolution fusion | flops 2568585216 | bytes 11403264 | tf_op jit(solution)/shard_map/dot_general | solution.py:351
  109.9 7.9 %conv_backward_3.1 = (bf16[512,384]{1,0:T(8,128)(2,1)}, bf16[512,384]{1,0:T(8,128)(2,1)}, bf16[512,1536]{1,0:T(8,128)(2,1)}, bf16[512,1536]{1,0:T(8,128)(2,1)}, f32[32,1536]{1,0:T(8,128)}) custom-call(s32[4]{0:T(128)} %pad_add_fusion.where_ref, bf16[544,1536]{1,0:T(8,128)(2,1)} %fusion.18.grad_ref, bf16[576,1536]{1,0:T(8,128)(2,1)} %get-tuple-element.154.glu_ref, ...), custom_call_target="tpu_custom_call" | custom-call | bytes 1024 | tf_op jit(solution)/shard_map/conv_backward_3/pallas_call | solution.py:219
  117.9 1.8 collective-permute-done.21
  120.8 2.1 fusion.21
  122.8 4.4 %convolution_convert_fusion = bf16[1536,1536]{1,0:T(8,128)(2,1)} fusion(bf16[512,1536]{1,0:T(8,128)(2,1)S(1)} %copy-done.28, bf16[512,1536]{1,0:T(8,128)(2,1)S(1)} %copy-done.8), kind=kOutput, calls=%fused_computation | convolution fusion | flops 2418278400 | bytes 7864320 | tf_op jit(solution)/shard_map/dot_general | solution.py:247
  127.3 7.9 %conv_backward_1.1 = (bf16[512,384]{1,0:T(8,128)(2,1)}, bf16[512,384]{1,0:T(8,128)(2,1)}, bf16[512,1536]{1,0:T(8,128)(2,1)}, bf16[512,1536]{1,0:T(8,128)(2,1)}, f32[32,1536]{1,0:T(8,128)}) custom-call(s32[4]{0:T(128)} %pad_add_fusion.where_ref, bf16[544,1536]{1,0:T(8,128)(2,1)} %fusion.18.grad_ref, ...), custom_call_target="tpu_custom_call", output_to_operand_aliasing={{2}: (6, {}), {3}: (7, {}), {4}: (8, {})} | custom-call | bytes 1024 | tf_op jit(solution)/shard_map/conv_backward_1/pallas_call | solution.py:219
  136.3 7.9 %conv_backward_2.1 = (bf16[512,384]{1,0:T(8,128)(2,1)}, bf16[512,384]{1,0:T(8,128)(2,1)}, bf16[512,1536]{1,0:T(8,128)(2,1)}, bf16[512,1536]{1,0:T(8,128)(2,1)}, f32[32,1536]{1,0:T(8,128)}) custom-call(s32[4]{0:T(128)} %pad_add_fusion.where_ref, bf16[544,1536]{1,0:T(8,128)(2,1)} %fusion.18.grad_ref, ...), custom_call_target="tpu_custom_call", output_to_operand_aliasing={{2}: (6, {}), {3}: (7, {}), {4}: (8, {})} | custom-call | bytes 1024 | tf_op jit(solution)/shard_map/conv_backward_2/pallas_call | solution.py:219
  145.3 2.1 fusion.22
  147.4 2.1 collective-permute-start.24
  149.5 8.0 %conv_backward_0.1 = (bf16[512,384]{1,0:T(8,128)(2,1)}, bf16[512,384]{1,0:T(8,128)(2,1)}, bf16[512,1536]{1,0:T(8,128)(2,1)}, bf16[512,1536]{1,0:T(8,128)(2,1)}, f32[32,1536]{1,0:T(8,128)}) custom-call(s32[4]{0:T(128)} %pad_add_fusion.where_ref, bf16[544,1536]{1,0:T(8,128)(2,1)} %fusion.18.grad_ref, ...), custom_call_target="tpu_custom_call", output_to_operand_aliasing={{2}: (6, {}), {3}: (7, {}), {4}: (8, {})} | custom-call | bytes 1024 | tf_op jit(solution)/shard_map/conv_backward_0/pallas_call | solution.py:219
  160.2 4.9 %fusion.37 = f32[512,1536]{1,0:T(8,128)S(1)} fusion(bf16[512,1536]{1,0:T(8,128)(2,1)S(1)} %copy-done.5, bf16[1536,1536]{1,0:T(8,128)(2,1)} %get-tuple-element.191), kind=kOutput, calls=%fused_computation.98 | convolution fusion | flops 2415919104 | bytes 9437184 | tf_op jit(solution)/shard_map/dot_general | solution.py:384
  165.2 3.2 %fusion.10 = (f32[512]{0:T(512)S(1)}, f32[1536]{0:T(1024)S(1)}, f32[512]{0:T(512)S(1)}, f32[512,1536]{1,0:T(8,128)S(1)}) fusion(bf16[1,512,1536]{2,1,0:T(8,128)(2,1)S(1)} %copy-done.3, f32[1536]{0:T(1024)S(1)} %copy-done.27, f32[512]{0:T(512)S(1)} %add_rsqrt_fusion, f32[512]{0:T(512)S(1)} %broadcast_multiply_fusion.2, f32[512,1536]{1,0:T(8,128)S(1)} %fusion.37, ...), kind=kOutput, calls=%fused_computation.17 | convolution fusion | flops 2423780864 | bytes 14176256 | tf_op jit(solution)/shard_map/dot_general | solution.py:382
  168.7 3.7 %fusion.19 = bf16[512,1536]{1,0:T(8,128)(2,1)} fusion(bf16[512,1536]{1,0:T(8,128)(2,1)S(1)} %copy-done.29, bf16[1536,1536]{1,0:T(8,128)(2,1)S(1)} %bitcast.121, bf16[1,512,1536]{2,1,0:T(8,128)(2,1)S(1)} %copy-done.3), kind=kOutput, calls=%fused_computation.30 | convolution fusion | flops 2418278400 | bytes 9437184 | tf_op jit(solution)/shard_map/dot_general | solution.py:387
  172.4 2.5 fusion.15
  175.9 14.3 %collective-permute-done.24 = bf16[1536,384]{1,0:T(8,128)(2,1)} collective-permute-done((bf16[1536,384]{1,0:T(8,128)(2,1)}, bf16[1536,384]{1,0:T(8,128)(2,1)}, u32[]{:S(2)}, u32[]{:S(2)}) %collective-permute-start.24) | collective-permute-done | bytes 1179680 | tf_op jit(solution)/shard_map/ppermute | solution.py:40
  190.2 3.0 %fusion.24 = bf16[1536,384]{1,0:T(8,128)(2,1)S(1)} fusion(f32[1536,384]{1,0:T(8,128)S(1)} %fusion.35, bf16[1536,512]{0,1:T(8,128)(2,1)S(1)} %bitcast.113, bf16[512,384]{1,0:T(8,128)(2,1)S(1)} %copy-done.14, bf16[1536,384]{1,0:T(8,128)(2,1)} %collective-permute-done.27, bf16[1536,384]{1,0:T(8,128)(2,1)S(1)} %collective-permute-done.26, ...), kind=kOutput, calls=%fused_computation.35 | convolution fusion | flops 608698368 | bytes 9043968 | tf_op jit(solution)/shard_map/dot_general | solution.py:359
  193.2 1.9 constant_dynamic-slice_fusion.1
  196.6 2.0 collective-permute-start.37
  199.6 2.6 collective-permute-done.35
  202.3 3.7 %collective-permute-start.31 = (bf16[384,384]{1,0:T(8,128)(2,1)S(1)}, bf16[384,384]{1,0:T(8,128)(2,1)S(1)}, u32[]{:S(2)}, u32[]{:S(2)}) collective-permute-start(bf16[384,384]{1,0:T(8,128)(2,1)S(1)} %get-tuple-element.222), channel_id=1, source_target_pairs={{0,6},{1,7},{2,0},{3,1},{4,2},{5,3},{6,4},{7,5},{8,14},{9,15},{10,... | collective-permute-start | bytes 884744 | tf_op jit(solution)/shard_map/ppermute | solution.py:40
  209.6 6.3 %collective-permute-done.33 = f32[32,1536]{1,0:T(8,128)S(1)} collective-permute-done((f32[32,1536]{1,0:T(8,128)S(1)}, f32[32,1536]{1,0:T(8,128)S(1)}, u32[]{:S(2)}, u32[]{:S(2)}) %collective-permute-start.33) | collective-permute-done | bytes 196640 | tf_op jit(solution)/shard_map/ppermute | solution.py:40
  215.9 4.0 %collective-permute-done.29 = bf16[384,384]{1,0:T(8,128)(2,1)S(1)} collective-permute-done((bf16[384,384]{1,0:T(8,128)(2,1)S(1)}, bf16[384,384]{1,0:T(8,128)(2,1)S(1)}, u32[]{:S(2)}, u32[]{:S(2)}) %collective-permute-start.29) | collective-permute-done | bytes 294944 | tf_op jit(solution)/shard_map/ppermute | solution.py:40
  219.9 2.1 collective-permute-done.31
  223.8 5.6 %collective-permute-start.45 = (f32[32,1536]{1,0:T(8,128)S(1)}, f32[32,1536]{1,0:T(8,128)S(1)}, u32[]{:S(2)}, u32[]{:S(2)}) collective-permute-start(f32[32,1536]{1,0:T(8,128)S(1)} %add_add_fusion), channel_id=1, source_target_pairs={{0,4},{1,5},{2,6},{3,7},{4,0},{5,1},{6,2},{7,3},{8,12},{9,13},{10,... | collective-permute-start | bytes 589832 | tf_op jit(solution)/shard_map/ppermute | solution.py:40
  231.7 1.4 collective-permute-start.43
  234.6 4.2 %collective-permute-done.45 = f32[32,1536]{1,0:T(8,128)S(1)} collective-permute-done((f32[32,1536]{1,0:T(8,128)S(1)}, f32[32,1536]{1,0:T(8,128)S(1)}, u32[]{:S(2)}, u32[]{:S(2)}) %collective-permute-start.45) | collective-permute-done | bytes 196640 | tf_op jit(solution)/shard_map/ppermute | solution.py:40
  238.8 2.0 collective-permute-start.41
  241.9 10.4 %collective-permute-done.44.refs_7_ = bf16[48,1536]{1,0:T(8,128)(2,1)S(1)} collective-permute-done((bf16[48,1536]{1,0:T(8,128)(2,1)S(1)}, bf16[48,1536]{1,0:T(8,128)(2,1)S(1)}, u32[]{:S(2)}, u32[]{:S(2)}) %collective-permute-start.44) | collective-permute-done | bytes 147488 | tf_op jit(solution)/shard_map/ppermute | solution.py:40
  254.3 3.4 %final.1 = (f32[192,3072]{1,0:T(8,128)}, f32[192,1536]{1,0:T(8,128)}) custom-call(s32[4]{0:T(128)} %pad_add_fusion.where_ref, bf16[2,192,384]{2,1,0:T(8,128)(2,1)} %copy-done.10, bf16[2,192,384]{2,1,0:T(8,128)(2,1)} %copy-done.18, bf16[2,192,384]{2,1,0:T(8,128)(2,1)} %copy-done.19, bf16[2,192,384]{2,1,0:T(8,128)(2,1)} %copy-done.20, ...), custom_call_target="tpu_custom_call" | custom-call | bytes 1024 | tf_op jit(solution)/shard_map/final/pallas_call | solution.py:267
  (193 shorter events, 48.5 us)
Async XLA Ops:
  7.2 94.9 %all-gather.2.cloned.1.call-start = ((), (), s32[]{:S(2)}) async-start(), calls=%async_computation.1 | async-start | bytes 5308416 | tf_op jit(solution)/shard_map/all_gather | solution.py:331
  8.4 26.5 %collective-permute-start = (bf16[2,192,384]{2,1,0:T(8,128)(2,1)S(1)}, bf16[2,192,384]{2,1,0:T(8,128)(2,1)}, u32[]{:S(2)}, u32[]{:S(2)}) collective-permute-start(bf16[2,192,384]{2,1,0:T(8,128)(2,1)S(1)} %pad_maximum_fusion.4), channel_id=1, source_target_pairs={{0,2},{1,3},{2,4},{3,5},{4,6},{5,7},{6,0},{7,1},{8,10},{9,11},{10,... | collective-permute-start | bytes 884744 | tf_op jit(solution)/shard_map/ppermute | solution.py:40
  11.5 24.5 %collective-permute-start.1 = (bf16[2,192,384]{2,1,0:T(8,128)(2,1)S(1)}, bf16[2,192,384]{2,1,0:T(8,128)(2,1)}, u32[]{:S(2)}, u32[]{:S(2)}) collective-permute-start(bf16[2,192,384]{2,1,0:T(8,128)(2,1)S(1)} %pad_maximum_fusion.4), channel_id=1, source_target_pairs={{0,6},{1,7},{2,0},{3,1},{4,2},{5,3},{6,4},{7,5},{8,14},{9,15},{10,... | collective-permute-start | bytes 884744 | tf_op jit(solution)/shard_map/ppermute | solution.py:40
  13.6 26.0 %collective-permute-start.2 = (bf16[2,192,384]{2,1,0:T(8,128)(2,1)S(1)}, bf16[2,192,384]{2,1,0:T(8,128)(2,1)}, u32[]{:S(2)}, u32[]{:S(2)}) collective-permute-start(bf16[2,192,384]{2,1,0:T(8,128)(2,1)S(1)} %pad_maximum_fusion.4), channel_id=1, source_target_pairs={{0,4},{1,5},{2,6},{3,7},{4,0},{5,1},{6,2},{7,3},{8,12},{9,13},{10,... | collective-permute-start | bytes 884744 | tf_op jit(solution)/shard_map/ppermute | solution.py:40
  17.0 10.0 %collective-permute-start.3 = (bf16[48,1536]{1,0:T(8,128)(2,1)}, bf16[48,1536]{1,0:T(8,128)(2,1)}, u32[]{:S(2)}, u32[]{:S(2)}) collective-permute-start(bf16[48,1536]{1,0:T(8,128)(2,1)} %pad_maximum_fusion.8), channel_id=1, source_target_pairs={{0,8},{8,16},{16,24},{1,9},{9,17},{17,25},{2,10},{10,18},{18,26},{... | collective-permute-start | bytes 442376 | tf_op jit(solution)/shard_map/ppermute | solution.py:243
  21.7 7.3 %collective-permute-start.4 = (bf16[48,1536]{1,0:T(8,128)(2,1)}, bf16[48,1536]{1,0:T(8,128)(2,1)}, u32[]{:S(2)}, u32[]{:S(2)}) collective-permute-start(bf16[48,1536]{1,0:T(8,128)(2,1)} %pad_maximum_fusion.9), channel_id=1, source_target_pairs={{8,0},{16,8},{24,16},{9,1},{17,9},{25,17},{10,2},{18,10},{26,18},{... | collective-permute-start | bytes 442376 | tf_op jit(solution)/shard_map/ppermute | solution.py:243
  27.0 14.6 %collective-permute-start.5 = (bf16[192,3072]{1,0:T(8,128)(2,1)S(1)}, bf16[192,3072]{1,0:T(8,128)(2,1)S(1)}, u32[]{:S(2)}, u32[]{:S(2)}) collective-permute-start(bf16[192,3072]{1,0:T(8,128)(2,1)S(1)} %copy-done), channel_id=1, source_target_pairs={{0,1},{1,0},{2,3},{3,2},{4,5},{5,4},{6,7},{7,6},{8,9},{9,8},{10,11... | collective-permute-start | bytes 3538952 | tf_op jit(solution)/shard_map/ppermute | solution.py:40
  42.7 150.6 %reduce-scatter.2.cloned.1.call-start = ((), (), s32[]{:S(2)}) async-start(), calls=%async_computation.2 | async-start | bytes 5308416 | tf_op jit(solution)/shard_map/reduce_scatter | solution.py:371
  42.7 13.9 %collective-permute-start.6 = (bf16[512,1536]{1,0:T(8,128)(2,1)S(1)}, bf16[512,1536]{1,0:T(8,128)(2,1)S(1)}, u32[]{:S(2)}, u32[]{:S(2)}) collective-permute-start(bf16[512,1536]{1,0:T(8,128)(2,1)S(1)} %get-tuple-element.110), channel_id=1, source_target_pairs={{0,1},{1,0},{2,3},{3,2},{4,5},{5,4},{6,7},{7,6},{8,9},{9,8},{10,11... | collective-permute-start | bytes 4718600 | tf_op jit(solution)/shard_map/ppermute | solution.py:40
  42.8 4.0 %collective-permute-start.7 = (bf16[3,2,96,384]{3,2,1,0:T(8,128)(2,1)}, bf16[3,2,96,384]{3,2,1,0:T(8,128)(2,1)}, u32[]{:S(2)}, u32[]{:S(2)}) collective-permute-start(bf16[3,2,96,384]{3,2,1,0:T(8,128)(2,1)} %get-tuple-element.113.refs_4_), channel_id=1, source_target_pairs={{0,1},{1,0},{2,3},{3,2},{4,5},{5,4},{6,7},{7,6},{8,9},{9,8},{10,11... | collective-permute-start | bytes 1327112 | tf_op jit(solution)/shard_map/ppermute | solution.py:40
  43.3 5.1 %collective-permute-start.8 = (bf16[3,2,96,384]{3,2,1,0:T(8,128)(2,1)}, bf16[3,2,96,384]{3,2,1,0:T(8,128)(2,1)}, u32[]{:S(2)}, u32[]{:S(2)}) collective-permute-start(bf16[3,2,96,384]{3,2,1,0:T(8,128)(2,1)} %get-tuple-element.114.refs_5_), channel_id=1, source_target_pairs={{0,1},{1,0},{2,3},{3,2},{4,5},{5,4},{6,7},{7,6},{8,9},{9,8},{10,11... | collective-permute-start | bytes 1327112 | tf_op jit(solution)/shard_map/ppermute | solution.py:40
  43.4 13.3 %collective-permute-start.10 = (bf16[3,2,96,384]{3,2,1,0:T(8,128)(2,1)}, bf16[3,2,96,384]{3,2,1,0:T(8,128)(2,1)}, u32[]{:S(2)}, u32[]{:S(2)}) collective-permute-start(bf16[3,2,96,384]{3,2,1,0:T(8,128)(2,1)} %get-tuple-element.114.refs_5_), channel_id=1, source_target_pairs={{0,16},{1,17},{2,18},{3,19},{4,20},{5,21},{6,22},{7,23},{8,24},{9,... | collective-permute-start | bytes 1327112 | tf_op jit(solution)/shard_map/ppermute | solution.py:40
  44.9 13.3 %collective-permute-start.11 = (bf16[3,2,96,384]{3,2,1,0:T(8,128)(2,1)}, bf16[3,2,96,384]{3,2,1,0:T(8,128)(2,1)}, u32[]{:S(2)}, u32[]{:S(2)}) collective-permute-start(bf16[3,2,96,384]{3,2,1,0:T(8,128)(2,1)} %get-tuple-element.114.refs_5_), channel_id=1, source_target_pairs={{0,8},{1,9},{2,10},{3,11},{4,12},{5,13},{6,14},{7,15},{8,0},{9,1},... | collective-permute-start | bytes 1327112 | tf_op jit(solution)/shard_map/ppermute | solution.py:40
  46.8 18.9 %collective-permute-start.12 = (bf16[3,2,96,384]{3,2,1,0:T(8,128)(2,1)}, bf16[3,2,96,384]{3,2,1,0:T(8,128)(2,1)}, u32[]{:S(2)}, u32[]{:S(2)}) collective-permute-start(bf16[3,2,96,384]{3,2,1,0:T(8,128)(2,1)} %get-tuple-element.113.refs_4_), channel_id=1, source_target_pairs={{0,16},{1,17},{2,18},{3,19},{4,20},{5,21},{6,22},{7,23},{8,24},{9,... | collective-permute-start | bytes 1327112 | tf_op jit(solution)/shard_map/ppermute | solution.py:40
  48.4 18.6 %collective-permute-start.9 = (bf16[3,2,96,384]{3,2,1,0:T(8,128)(2,1)}, bf16[3,2,96,384]{3,2,1,0:T(8,128)(2,1)}, u32[]{:S(2)}, u32[]{:S(2)}) collective-permute-start(bf16[3,2,96,384]{3,2,1,0:T(8,128)(2,1)} %get-tuple-element.113.refs_4_), channel_id=1, source_target_pairs={{0,8},{1,9},{2,10},{3,11},{4,12},{5,13},{6,14},{7,15},{8,0},{9,1},... | collective-permute-start | bytes 1327112 | tf_op jit(solution)/shard_map/ppermute | solution.py:40
  66.9 2.1 collective-permute-start.17
  66.9 3.6 %collective-permute-start.18 = (bf16[3,2,96,384]{3,2,1,0:T(8,128)(2,1)}, bf16[3,2,96,384]{3,2,1,0:T(8,128)(2,1)}, u32[]{:S(2)}, u32[]{:S(2)}) collective-permute-start(bf16[3,2,96,384]{3,2,1,0:T(8,128)(2,1)} %collective-permute-done.11.refs_5_), channel_id=1, source_target_pairs={{0,1},{1,0},{2,3},{3,2},{4,5},{5,4},{6,7},{7,6},{8,9},{9,8},{10,11... | collective-permute-start | bytes 1327112 | tf_op jit(solution)/shard_map/ppermute | solution.py:40
  67.5 9.3 %collective-permute-start.15 = (bf16[3,2,96,384]{3,2,1,0:T(8,128)(2,1)}, bf16[3,2,96,384]{3,2,1,0:T(8,128)(2,1)}, u32[]{:S(2)}, u32[]{:S(2)}) collective-permute-start(bf16[3,2,96,384]{3,2,1,0:T(8,128)(2,1)} %collective-permute-done.12.refs_4_), channel_id=1, source_target_pairs={{0,1},{1,0},{2,3},{3,2},{4,5},{5,4},{6,7},{7,6},{8,9},{9,8},{10,11... | collective-permute-start | bytes 1327112 | tf_op jit(solution)/shard_map/ppermute | solution.py:40
  67.5 9.3 %collective-permute-start.16 = (bf16[3,2,96,384]{3,2,1,0:T(8,128)(2,1)}, bf16[3,2,96,384]{3,2,1,0:T(8,128)(2,1)}, u32[]{:S(2)}, u32[]{:S(2)}) collective-permute-start(bf16[3,2,96,384]{3,2,1,0:T(8,128)(2,1)} %collective-permute-done.10.refs_5_), channel_id=1, source_target_pairs={{0,1},{1,0},{2,3},{3,2},{4,5},{5,4},{6,7},{7,6},{8,9},{9,8},{10,11... | collective-permute-start | bytes 1327112 | tf_op jit(solution)/shard_map/ppermute | solution.py:40
  68.0 14.9 %collective-permute-start.13 = (bf16[3,2,96,384]{3,2,1,0:T(8,128)(2,1)}, bf16[3,2,96,384]{3,2,1,0:T(8,128)(2,1)S(1)}, u32[]{:S(2)}, u32[]{:S(2)}) collective-permute-start(bf16[3,2,96,384]{3,2,1,0:T(8,128)(2,1)} %collective-permute-done.9.refs_4_), channel_id=1, source_target_pairs={{0,16},{1,17},{2,18},{3,19},{4,20},{5,21},{6,22},{7,23},{8,24},{9,... | collective-permute-start | bytes 1327112 | tf_op jit(solution)/shard_map/ppermute | solution.py:40
  69.1 13.8 %collective-permute-start.14 = (bf16[3,2,96,384]{3,2,1,0:T(8,128)(2,1)}, bf16[3,2,96,384]{3,2,1,0:T(8,128)(2,1)}, u32[]{:S(2)}, u32[]{:S(2)}) collective-permute-start(bf16[3,2,96,384]{3,2,1,0:T(8,128)(2,1)} %collective-permute-done.10.refs_5_), channel_id=1, source_target_pairs={{0,8},{1,9},{2,10},{3,11},{4,12},{5,13},{6,14},{7,15},{8,0},{9,1},... | collective-permute-start | bytes 1327112 | tf_op jit(solution)/shard_map/ppermute | solution.py:40
  82.9 1.9 collective-permute-start.19
  83.0 2.8 %collective-permute-start.20 = (bf16[3,2,96,384]{3,2,1,0:T(8,128)(2,1)}, bf16[3,2,96,384]{3,2,1,0:T(8,128)(2,1)}, u32[]{:S(2)}, u32[]{:S(2)}) collective-permute-start(bf16[3,2,96,384]{3,2,1,0:T(8,128)(2,1)} %collective-permute-done.14.refs_5_), channel_id=1, source_target_pairs={{0,1},{1,0},{2,3},{3,2},{4,5},{5,4},{6,7},{7,6},{8,9},{9,8},{10,11... | collective-permute-start | bytes 1327112 | tf_op jit(solution)/shard_map/ppermute | solution.py:40
  117.8 1.9 collective-permute-start.21
  135.2 9.1 %collective-permute-start.22 = (bf16[512,384]{1,0:T(8,128)(2,1)}, bf16[512,384]{1,0:T(8,128)(2,1)S(1)}, u32[]{:S(2)}, u32[]{:S(2)}) collective-permute-start(bf16[512,384]{1,0:T(8,128)(2,1)} %get-tuple-element.177), channel_id=1, source_target_pairs={{0,1},{1,0},{2,3},{3,2},{4,5},{5,4},{6,7},{7,6},{8,9},{9,8},{10,11... | collective-permute-start | bytes 1179656 | tf_op jit(solution)/shard_map/ppermute | solution.py:40
  135.3 54.8 %collective-permute-start.27 = (bf16[1536,384]{1,0:T(8,128)(2,1)}, bf16[1536,384]{1,0:T(8,128)(2,1)}, u32[]{:S(2)}, u32[]{:S(2)}) collective-permute-start(bf16[1536,384]{1,0:T(8,128)(2,1)} %fusion.21), channel_id=1, source_target_pairs={{0,24},{1,25},{2,26},{3,27},{4,28},{5,29},{6,30},{7,31},{8,16},{9,... | collective-permute-start | bytes 3538952 | tf_op jit(solution)/shard_map/ppermute | solution.py:40
  144.3 13.4 %collective-permute-start.25 = (bf16[512,384]{1,0:T(8,128)(2,1)}, bf16[512,384]{1,0:T(8,128)(2,1)S(1)}, u32[]{:S(2)}, u32[]{:S(2)}) collective-permute-start(bf16[512,384]{1,0:T(8,128)(2,1)} %get-tuple-element.184), channel_id=1, source_target_pairs={{0,1},{1,0},{2,3},{3,2},{4,5},{5,4},{6,7},{7,6},{8,9},{9,8},{10,11... | collective-permute-start | bytes 1179656 | tf_op jit(solution)/shard_map/ppermute | solution.py:40
  147.4 42.8 %collective-permute-start.24 = (bf16[1536,384]{1,0:T(8,128)(2,1)}, bf16[1536,384]{1,0:T(8,128)(2,1)}, u32[]{:S(2)}, u32[]{:S(2)}) collective-permute-start(bf16[1536,384]{1,0:T(8,128)(2,1)} %fusion.22), channel_id=1, source_target_pairs={{0,8},{1,9},{2,10},{3,11},{4,12},{5,13},{6,14},{7,15},{8,0},{9,1},... | collective-permute-start | bytes 3538952 | tf_op jit(solution)/shard_map/ppermute | solution.py:40
  157.5 17.4 %collective-permute-start.23 = (bf16[512,384]{1,0:T(8,128)(2,1)}, bf16[512,384]{1,0:T(8,128)(2,1)S(1)}, u32[]{:S(2)}, u32[]{:S(2)}) collective-permute-start(bf16[512,384]{1,0:T(8,128)(2,1)} %get-tuple-element.182), channel_id=1, source_target_pairs={{0,1},{1,0},{2,3},{3,2},{4,5},{5,4},{6,7},{7,6},{8,9},{9,8},{10,11... | collective-permute-start | bytes 1179656 | tf_op jit(solution)/shard_map/ppermute | solution.py:40
  159.7 30.4 %collective-permute-start.26 = (bf16[1536,384]{1,0:T(8,128)(2,1)S(1)}, bf16[1536,384]{1,0:T(8,128)(2,1)S(1)}, u32[]{:S(2)}, u32[]{:S(2)}) collective-permute-start(bf16[1536,384]{1,0:T(8,128)(2,1)S(1)} %fusion.23), channel_id=1, source_target_pairs={{0,16},{1,17},{2,18},{3,19},{4,20},{5,21},{6,22},{7,23},{8,24},{9,... | collective-permute-start | bytes 3538952 | tf_op jit(solution)/shard_map/ppermute | solution.py:40
  168.5 7.4 %collective-permute-start.28 = (f32[32,1536]{1,0:T(8,128)S(1)}, f32[32,1536]{1,0:T(8,128)S(1)}, u32[]{:S(2)}, u32[]{:S(2)}) collective-permute-start(f32[32,1536]{1,0:T(8,128)S(1)} %pad_maximum_fusion.7), channel_id=1, source_target_pairs={{0,1},{1,0},{2,3},{3,2},{4,5},{5,4},{6,7},{7,6},{8,9},{9,8},{10,11... | collective-permute-start | bytes 589832 | tf_op jit(solution)/shard_map/ppermute | solution.py:40
  195.1 7.0 %collective-permute-start.35 = (bf16[48,1536]{1,0:T(8,128)(2,1)}, bf16[48,1536]{1,0:T(8,128)(2,1)}, u32[]{:S(2)}, u32[]{:S(2)}) collective-permute-start(bf16[48,1536]{1,0:T(8,128)(2,1)} %get-tuple-element.229), channel_id=1, source_target_pairs={{0,8},{1,9},{2,10},{3,11},{4,12},{5,13},{6,14},{7,15},{8,0},{9,1},... | collective-permute-start | bytes 442376 | tf_op jit(solution)/shard_map/ppermute | solution.py:40
  195.9 6.4 %collective-permute-start.36 = (bf16[48,1536]{1,0:T(8,128)(2,1)}, bf16[48,1536]{1,0:T(8,128)(2,1)}, u32[]{:S(2)}, u32[]{:S(2)}) collective-permute-start(bf16[48,1536]{1,0:T(8,128)(2,1)} %get-tuple-element.228), channel_id=1, source_target_pairs={{0,16},{1,17},{2,18},{3,19},{4,20},{5,21},{6,22},{7,23},{8,24},{9,... | collective-permute-start | bytes 442376 | tf_op jit(solution)/shard_map/ppermute | solution.py:40
  196.6 9.4 %collective-permute-start.37 = (bf16[48,1536]{1,0:T(8,128)(2,1)S(1)}, bf16[48,1536]{1,0:T(8,128)(2,1)S(1)}, u32[]{:S(2)}, u32[]{:S(2)}) collective-permute-start(bf16[48,1536]{1,0:T(8,128)(2,1)S(1)} %get-tuple-element.227), channel_id=1, source_target_pairs={{0,24},{1,25},{2,26},{3,27},{4,28},{5,29},{6,30},{7,31},{8,16},{9,... | collective-permute-start | bytes 442376 | tf_op jit(solution)/shard_map/ppermute | solution.py:40
  198.6 9.8 %collective-permute-start.32 = (f32[32,1536]{1,0:T(8,128)S(1)}, f32[32,1536]{1,0:T(8,128)S(1)}, u32[]{:S(2)}, u32[]{:S(2)}) collective-permute-start(f32[32,1536]{1,0:T(8,128)S(1)} %fusion.64), channel_id=1, source_target_pairs={{0,8},{1,9},{2,10},{3,11},{4,12},{5,13},{6,14},{7,15},{8,0},{9,1},... | collective-permute-start | bytes 589832 | tf_op jit(solution)/shard_map/ppermute | solution.py:40
  199.5 20.5 %collective-permute-start.29 = (bf16[384,384]{1,0:T(8,128)(2,1)S(1)}, bf16[384,384]{1,0:T(8,128)(2,1)S(1)}, u32[]{:S(2)}, u32[]{:S(2)}) collective-permute-start(bf16[384,384]{1,0:T(8,128)(2,1)S(1)} %get-tuple-element.224), channel_id=1, source_target_pairs={{0,4},{1,5},{2,6},{3,7},{4,0},{5,1},{6,2},{7,3},{8,12},{9,13},{10,... | collective-permute-start | bytes 884744 | tf_op jit(solution)/shard_map/ppermute | solution.py:40
  202.2 17.8 %collective-permute-start.30 = (bf16[384,384]{1,0:T(8,128)(2,1)S(1)}, bf16[384,384]{1,0:T(8,128)(2,1)S(1)}, u32[]{:S(2)}, u32[]{:S(2)}) collective-permute-start(bf16[384,384]{1,0:T(8,128)(2,1)S(1)} %get-tuple-element.223), channel_id=1, source_target_pairs={{0,2},{1,3},{2,4},{3,5},{4,6},{5,7},{6,0},{7,1},{8,10},{9,11},{10,... | collective-permute-start | bytes 884744 | tf_op jit(solution)/shard_map/ppermute | solution.py:40
  202.3 19.7 %collective-permute-start.31 = (bf16[384,384]{1,0:T(8,128)(2,1)S(1)}, bf16[384,384]{1,0:T(8,128)(2,1)S(1)}, u32[]{:S(2)}, u32[]{:S(2)}) collective-permute-start(bf16[384,384]{1,0:T(8,128)(2,1)S(1)} %get-tuple-element.222), channel_id=1, source_target_pairs={{0,6},{1,7},{2,0},{3,1},{4,2},{5,3},{6,4},{7,5},{8,14},{9,15},{10,... | collective-permute-start | bytes 884744 | tf_op jit(solution)/shard_map/ppermute | solution.py:40
  206.0 9.9 %collective-permute-start.33 = (f32[32,1536]{1,0:T(8,128)S(1)}, f32[32,1536]{1,0:T(8,128)S(1)}, u32[]{:S(2)}, u32[]{:S(2)}) collective-permute-start(f32[32,1536]{1,0:T(8,128)S(1)} %fusion.64), channel_id=1, source_target_pairs={{0,16},{1,17},{2,18},{3,19},{4,20},{5,21},{6,22},{7,23},{8,24},{9,... | collective-permute-start | bytes 589832 | tf_op jit(solution)/shard_map/ppermute | solution.py:40
  208.4 7.5 %collective-permute-start.34 = (f32[32,1536]{1,0:T(8,128)S(1)}, f32[32,1536]{1,0:T(8,128)S(1)}, u32[]{:S(2)}, u32[]{:S(2)}) collective-permute-start(f32[32,1536]{1,0:T(8,128)S(1)} %fusion.64), channel_id=1, source_target_pairs={{0,24},{1,25},{2,26},{3,27},{4,28},{5,29},{6,30},{7,31},{8,16},{9,... | collective-permute-start | bytes 589832 | tf_op jit(solution)/shard_map/ppermute | solution.py:40
  223.8 15.0 %collective-permute-start.45 = (f32[32,1536]{1,0:T(8,128)S(1)}, f32[32,1536]{1,0:T(8,128)S(1)}, u32[]{:S(2)}, u32[]{:S(2)}) collective-permute-start(f32[32,1536]{1,0:T(8,128)S(1)} %add_add_fusion), channel_id=1, source_target_pairs={{0,4},{1,5},{2,6},{3,7},{4,0},{5,1},{6,2},{7,3},{8,12},{9,13},{10,... | collective-permute-start | bytes 589832 | tf_op jit(solution)/shard_map/ppermute | solution.py:40
  230.5 10.4 %collective-permute-start.42 = (bf16[48,1536]{1,0:T(8,128)(2,1)S(1)}, bf16[48,1536]{1,0:T(8,128)(2,1)S(1)}, u32[]{:S(2)}, u32[]{:S(2)}) collective-permute-start(bf16[48,1536]{1,0:T(8,128)(2,1)S(1)} %add_convert_fusion.1.refs_4_), channel_id=1, source_target_pairs={{0,8},{1,9},{2,10},{3,11},{4,12},{5,13},{6,14},{7,15},{8,0},{9,1},... | collective-permute-start | bytes 442376 | tf_op jit(solution)/shard_map/ppermute | solution.py:40
  231.7 9.3 %collective-permute-start.43 = (bf16[48,1536]{1,0:T(8,128)(2,1)S(1)}, bf16[48,1536]{1,0:T(8,128)(2,1)S(1)}, u32[]{:S(2)}, u32[]{:S(2)}) collective-permute-start(bf16[48,1536]{1,0:T(8,128)(2,1)S(1)} %add_convert_fusion.1.refs_4_), channel_id=1, source_target_pairs={{0,16},{1,17},{2,18},{3,19},{4,20},{5,21},{6,22},{7,23},{8,24},{9,... | collective-permute-start | bytes 442376 | tf_op jit(solution)/shard_map/ppermute | solution.py:40
  233.1 19.2 %collective-permute-start.39 = (bf16[2,192,384]{2,1,0:T(8,128)(2,1)S(1)}, bf16[2,192,384]{2,1,0:T(8,128)(2,1)S(1)}, u32[]{:S(2)}, u32[]{:S(2)}) collective-permute-start(bf16[2,192,384]{2,1,0:T(8,128)(2,1)S(1)} %pad_maximum_fusion.5.refs_0_), channel_id=1, source_target_pairs={{0,8},{1,9},{2,10},{3,11},{4,12},{5,13},{6,14},{7,15},{8,0},{9,1},... | collective-permute-start | bytes 884744 | tf_op jit(solution)/shard_map/ppermute | solution.py:40
  233.4 19.4 %collective-permute-start.40 = (bf16[2,192,384]{2,1,0:T(8,128)(2,1)S(1)}, bf16[2,192,384]{2,1,0:T(8,128)(2,1)S(1)}, u32[]{:S(2)}, u32[]{:S(2)}) collective-permute-start(bf16[2,192,384]{2,1,0:T(8,128)(2,1)S(1)} %pad_maximum_fusion.5.refs_0_), channel_id=1, source_target_pairs={{0,16},{1,17},{2,18},{3,19},{4,20},{5,21},{6,22},{7,23},{8,24},{9,... | collective-permute-start | bytes 884744 | tf_op jit(solution)/shard_map/ppermute | solution.py:40
  238.8 14.0 %collective-permute-start.41 = (bf16[2,192,384]{2,1,0:T(8,128)(2,1)S(1)}, bf16[2,192,384]{2,1,0:T(8,128)(2,1)S(1)}, u32[]{:S(2)}, u32[]{:S(2)}) collective-permute-start(bf16[2,192,384]{2,1,0:T(8,128)(2,1)S(1)} %pad_maximum_fusion.5.refs_0_), channel_id=1, source_target_pairs={{0,24},{1,25},{2,26},{3,27},{4,28},{5,29},{6,30},{7,31},{8,16},{9,... | collective-permute-start | bytes 884744 | tf_op jit(solution)/shard_map/ppermute | solution.py:40
  240.9 16.8 %collective-permute-start.46 = (f32[32,1536]{1,0:T(8,128)S(1)}, f32[32,1536]{1,0:T(8,128)S(1)}, u32[]{:S(2)}, u32[]{:S(2)}) collective-permute-start(f32[32,1536]{1,0:T(8,128)S(1)} %add.206), channel_id=1, source_target_pairs={{0,2},{1,3},{2,4},{3,5},{4,6},{5,7},{6,0},{7,1},{8,10},{9,11},{10,... | collective-permute-start | bytes 589832 | tf_op jit(solution)/shard_map/ppermute | solution.py:40
  241.0 11.4 %collective-permute-start.44 = (bf16[48,1536]{1,0:T(8,128)(2,1)S(1)}, bf16[48,1536]{1,0:T(8,128)(2,1)S(1)}, u32[]{:S(2)}, u32[]{:S(2)}) collective-permute-start(bf16[48,1536]{1,0:T(8,128)(2,1)S(1)} %add_convert_fusion.1.refs_4_), channel_id=1, source_target_pairs={{0,24},{1,25},{2,26},{3,27},{4,28},{5,29},{6,30},{7,31},{8,16},{9,... | collective-permute-start | bytes 442376 | tf_op jit(solution)/shard_map/ppermute | solution.py:40
  (35 other events, 219.0 us)
Sparse Core Ops, SparseCore 0:
  42.8 50.9 all-gather.1
  127.4 53.1 reduce-scatter.1
